TPU v7x, 32 devices: a whole 2x2x4 slice. The times are simulated.
32 devices in a mesh: dp: 32 (over z, y, x, core).
Axes of the slice: x: 2, y: 2, z: 4, core: 2. Of those that a mesh axis runs over, the one named last changes fastest.
Arguments:
- text: bfloat16 [768, 40, 768], P('dp'), may hold values from -6 to 6
- patches: bfloat16 [384, 145, 1024], P('dp'), may hold values from -6 to 6
- segment_ids: int32 [768, 40], P('dp'), may hold values from 0 to 7, never falling along the last dimension, each value on 1 to 10 neighbouring positions
- row_image: int32 [768], P('dp'), may hold values from 0 to 11
- self_query: bfloat16 [768, 768], P(None, 'dp'), may hold values from -0.21875 to 0.21875
- self_key: bfloat16 [768, 768], P(None, 'dp'), may hold values from -0.21875 to 0.21875
- self_value: bfloat16 [768, 768], P(None, 'dp'), may hold values from -0.21875 to 0.21875
- self_out: bfloat16 [768, 768], P(None, 'dp'), may hold values from -0.3125 to 0.3125
- cross_query: bfloat16 [768, 768], P(None, 'dp'), may hold values from -0.21875 to 0.21875
- cross_key: bfloat16 [1024, 768], P(None, 'dp'), may hold values from -0.1875 to 0.1875
- cross_value: bfloat16 [1024, 768], P(None, 'dp'), may hold values from -0.1875 to 0.1875
- cross_out: bfloat16 [768, 768], P(None, 'dp'), may hold values from -0.875 to 0.875
- ffn_up: bfloat16 [768, 3072], P(None, 'dp'), may hold values from -0.21875 to 0.21875
- ffn_down: bfloat16 [3072, 768], P(None, 'dp'), may hold values from -0.109375 to 0.109375
- norm_params: bfloat16 [6, 768], P(None, 'dp'), may hold values from -2 to 2, as said below
- cotangent: float32 [768, 40, 768], P('dp'), may hold values from -6 to 6
Outputs:
- output: float32 [768, 40, 768], P('dp')
- text_grad: float32 [768, 40, 768], P('dp')
- patch_grad: float32 [384, 145, 1024], P('dp')
- self_query_grad: float32 [768, 768], P(None, 'dp')
- self_key_grad: float32 [768, 768], P(None, 'dp')
- self_value_grad: float32 [768, 768], P(None, 'dp')
- self_out_grad: float32 [768, 768], P(None, 'dp')
- cross_query_grad: float32 [768, 768], P(None, 'dp')
- cross_key_grad: float32 [1024, 768], P(None, 'dp')
- cross_value_grad: float32 [1024, 768], P(None, 'dp')
- cross_out_grad: float32 [768, 768], P(None, 'dp')
- ffn_up_grad: float32 [768, 3072], P(None, 'dp')
- ffn_down_grad: float32 [3072, 768], P(None, 'dp')
- norm_grad: float32 [6, 768], P(None, 'dp')
Inputs may be any that keep to these rules, and one draw needn't show every extreme that they name: `segment_ids`: along each packed row the phrase ids never fall; each phrase holds 1 to 10 tokens, and one holds exactly 10. Row r uses image (r // 24) * 12 + row_image[r]. `norm_params`: gain rows are positive.
All inputs are finite; a program needn't handle non-finite values.
Results may differ from a plain program's by a relative error of at most 0.019.
Values may be sent and summed in bfloat16 or wider, within the bound.
A program may use at most 320 MiB of HBM per device.

v0:
```python
import jax
import jax.numpy as jnp
from jax import lax
from jax.sharding import PartitionSpec as P

HEADS = 12
HD = 64


masked_score = -1e30
epsilon = 1e-06


def project(left, right):
    return jnp.dot(left, right, preferred_element_type=jnp.float32)


def project_back(left, right):
    return lax.dot_general(
        left, right, (((1,), (1,)), ((), ())), preferred_element_type=jnp.float32
    )


def outer_sum(left, right):
    return lax.dot_general(
        left, right, (((0,), (0,)), ((), ())), preferred_element_type=jnp.float32
    )


def exact_gelu(values):
    return jax.nn.gelu(values, approximate=False)


def normalize(residual, gain, shift):
    average = jnp.mean(residual, axis=-1, keepdims=True)
    centered = residual - average
    inverse = lax.rsqrt(jnp.mean(centered * centered, axis=-1, keepdims=True) + epsilon)
    normed = centered * inverse
    return (normed * gain + shift, normed, inverse)


def normalize_back(grad_out, normed, inverse, gain):
    scaled = grad_out * gain
    return inverse * (
        scaled
        - jnp.mean(scaled, axis=-1, keepdims=True)
        - normed * jnp.mean(scaled * normed, axis=-1, keepdims=True)
    )


def norm_terms(grad_out, normed):
    return jnp.stack([jnp.sum(grad_out * normed, axis=0), jnp.sum(grad_out, axis=0)])


def scores_of(queries, key_rows, allowed):
    scores = (
        jnp.einsum("rqhe,rkhe->rhqk", queries, key_rows, preferred_element_type=jnp.float32) * 0.125
    )
    if allowed is None:
        return scores
    return jnp.where(allowed, scores, masked_score)


def attend(queries, key_rows, value_rows, allowed):
    scores = scores_of(queries, key_rows, allowed)
    largest = jnp.max(scores, axis=-1, keepdims=True)
    exponent = jnp.exp(scores - largest)
    total = jnp.sum(exponent, axis=-1, keepdims=True)
    weights = (exponent / total).astype(jnp.bfloat16)
    attended = jnp.einsum(
        "rhqk,rkhe->rqhe", weights, value_rows, preferred_element_type=jnp.float32
    )
    return (attended, largest + jnp.log(total))


def attend_back(queries, key_rows, value_rows, allowed, log_total, grad_out):
    weights = jnp.exp(scores_of(queries, key_rows, allowed) - log_total)
    grad_weights = jnp.einsum(
        "rqhe,rkhe->rhqk", grad_out, value_rows, preferred_element_type=jnp.float32
    )
    inner = jnp.sum(grad_weights * weights, axis=-1, keepdims=True)
    grad_scores = (weights * (grad_weights - inner) * 0.125).astype(jnp.bfloat16)
    grad_query = jnp.einsum(
        "rhqk,rkhe->rqhe", grad_scores, key_rows, preferred_element_type=jnp.float32
    )
    grad_key = jnp.einsum(
        "rhqk,rqhe->rkhe", grad_scores, queries, preferred_element_type=jnp.float32
    )
    grad_value = jnp.einsum(
        "rhqk,rqhe->rkhe",
        weights.astype(jnp.bfloat16),
        grad_out,
        preferred_element_type=jnp.float32,
    )
    return (grad_query, grad_key, grad_value)


def local(
    text,
    patches,
    segment_ids,
    row_image,
    self_query,
    self_key,
    self_value,
    self_out,
    cross_query,
    cross_key,
    cross_value,
    cross_out,
    ffn_up,
    ffn_down,
    norm_params,
    cotangent,
):
    gathered = (
        lax.all_gather(self_query, "dp", axis=1, tiled=True),
        lax.all_gather(self_key, "dp", axis=1, tiled=True),
        lax.all_gather(self_value, "dp", axis=1, tiled=True),
        lax.all_gather(self_out, "dp", axis=1, tiled=True),
        lax.all_gather(cross_query, "dp", axis=1, tiled=True),
        lax.all_gather(cross_key, "dp", axis=1, tiled=True),
        lax.all_gather(cross_value, "dp", axis=1, tiled=True),
        lax.all_gather(cross_out, "dp", axis=1, tiled=True),
        lax.all_gather(ffn_up, "dp", axis=1, tiled=True),
        lax.all_gather(ffn_down, "dp", axis=1, tiled=True),
        lax.all_gather(norm_params, "dp", axis=1, tiled=True),
    )
    (
        full_query,
        full_key,
        full_value,
        full_self_out,
        full_cross_query,
        full_cross_key,
        full_cross_value,
        full_cross_out,
        full_up,
        full_down,
        full_norm,
    ) = gathered
    gains = full_norm.astype(jnp.float32)
    row_count, length, width = text.shape
    image_count, patch_count, patch_width = patches.shape

    def split_rows(values):
        return values.reshape(row_count, -1, HEADS, HD)

    tokens = text.reshape(row_count * length, width)
    allowed = segment_ids[:, None, :, None] == segment_ids[:, None, None, :]
    query_self = project(tokens, full_query).astype(jnp.bfloat16)
    key_self = project(tokens, full_key).astype(jnp.bfloat16)
    value_self = project(tokens, full_value).astype(jnp.bfloat16)
    attended_self, total_self = attend(
        split_rows(query_self), split_rows(key_self), split_rows(value_self), allowed
    )
    mixed_self = attended_self.reshape(-1, width).astype(jnp.bfloat16)
    first, normed_one, inverse_one = normalize(
        tokens.astype(jnp.float32) + project(mixed_self, full_self_out), gains[0], gains[1]
    )
    first_low = first.astype(jnp.bfloat16)
    query_cross = project(first_low, full_cross_query).astype(jnp.bfloat16)
    patch_rows = patches.reshape(image_count * patch_count, patch_width)
    image_keys = (
        project(patch_rows, full_cross_key)
        .astype(jnp.bfloat16)
        .reshape(image_count, patch_count, HEADS, HD)
    )
    image_values = (
        project(patch_rows, full_cross_value)
        .astype(jnp.bfloat16)
        .reshape(image_count, patch_count, HEADS, HD)
    )
    key_rows = jnp.take(image_keys, row_image, axis=0)
    value_rows = jnp.take(image_values, row_image, axis=0)
    attended_cross, total_cross = attend(split_rows(query_cross), key_rows, value_rows, None)
    mixed_cross = attended_cross.reshape(-1, width).astype(jnp.bfloat16)
    second, normed_two, inverse_two = normalize(
        first + project(mixed_cross, full_cross_out), gains[2], gains[3]
    )
    second_low = second.astype(jnp.bfloat16)
    hidden_pre = project(second_low, full_up)
    activated, gelu_pullback = jax.vjp(exact_gelu, hidden_pre)
    hidden = activated.astype(jnp.bfloat16)
    output, normed_three, inverse_three = normalize(
        second + project(hidden, full_down), gains[4], gains[5]
    )
    (
        back_query,
        back_key,
        back_value,
        back_self_out,
        back_cross_query,
        back_cross_key,
        back_cross_value,
        back_cross_out,
        back_up,
        back_down,
        back_norm,
    ) = gathered
    back_gains = back_norm.astype(jnp.float32)
    grad_output = cotangent.reshape(-1, width)
    grad_three = normalize_back(grad_output, normed_three, inverse_three, back_gains[4])
    norm_three = norm_terms(grad_output, normed_three)
    branch_three = grad_three.astype(jnp.bfloat16)
    grad_down = outer_sum(hidden, branch_three)
    grad_hidden = project_back(branch_three, back_down)
    (grad_pre_full,) = gelu_pullback(grad_hidden)
    grad_pre = grad_pre_full.astype(jnp.bfloat16)
    grad_up = outer_sum(second_low, grad_pre)
    grad_second = grad_three + project_back(grad_pre, back_up)
    grad_two = normalize_back(grad_second, normed_two, inverse_two, back_gains[2])
    norm_two = norm_terms(grad_second, normed_two)
    branch_two = grad_two.astype(jnp.bfloat16)
    grad_cross_out = outer_sum(mixed_cross, branch_two)
    grad_mixed_cross = project_back(branch_two, back_cross_out).astype(jnp.bfloat16)
    grad_query_rows, grad_key_rows, grad_value_rows = attend_back(
        split_rows(query_cross),
        key_rows,
        value_rows,
        None,
        total_cross,
        split_rows(grad_mixed_cross),
    )
    chooser = (row_image[:, None] == jnp.arange(image_count, dtype=jnp.int32)[None, :]).astype(
        jnp.float32
    )
    grad_image_keys = jnp.einsum(
        "ri,rphe->iphe", chooser, grad_key_rows, precision=lax.Precision.HIGHEST
    )
    grad_image_values = jnp.einsum(
        "ri,rphe->iphe", chooser, grad_value_rows, precision=lax.Precision.HIGHEST
    )
    grad_image_keys = grad_image_keys.astype(jnp.bfloat16).reshape(image_count * patch_count, width)
    grad_image_values = grad_image_values.astype(jnp.bfloat16).reshape(
        image_count * patch_count, width
    )
    grad_cross_key = outer_sum(patch_rows, grad_image_keys)
    grad_cross_value = outer_sum(patch_rows, grad_image_values)
    patch_grad = (
        project_back(grad_image_keys, back_cross_key)
        + project_back(grad_image_values, back_cross_value)
    ).reshape(image_count, patch_count, patch_width)
    grad_query_cross = grad_query_rows.reshape(-1, width).astype(jnp.bfloat16)
    grad_cross_query = outer_sum(first_low, grad_query_cross)
    grad_first = grad_two + project_back(grad_query_cross, back_cross_query)
    grad_one = normalize_back(grad_first, normed_one, inverse_one, back_gains[0])
    norm_one = norm_terms(grad_first, normed_one)
    branch_one = grad_one.astype(jnp.bfloat16)
    grad_self_out = outer_sum(mixed_self, branch_one)
    grad_mixed_self = project_back(branch_one, back_self_out).astype(jnp.bfloat16)
    grad_query_self, grad_key_self, grad_value_self = attend_back(
        split_rows(query_self),
        split_rows(key_self),
        split_rows(value_self),
        allowed,
        total_self,
        split_rows(grad_mixed_self),
    )
    grad_query_low = grad_query_self.reshape(-1, width).astype(jnp.bfloat16)
    grad_key_low = grad_key_self.reshape(-1, width).astype(jnp.bfloat16)
    grad_value_low = grad_value_self.reshape(-1, width).astype(jnp.bfloat16)
    grad_self_query = outer_sum(tokens, grad_query_low)
    grad_self_key = outer_sum(tokens, grad_key_low)
    grad_self_value = outer_sum(tokens, grad_value_low)
    text_grad = (
        grad_one
        + project_back(grad_query_low, back_query)
        + project_back(grad_key_low, back_key)
        + project_back(grad_value_low, back_value)
    )
    norm_all = jnp.concatenate([norm_one, norm_two, norm_three], axis=0)
    shares = (
        lax.psum_scatter(grad_self_query, "dp", scatter_dimension=1, tiled=True),
        lax.psum_scatter(grad_self_key, "dp", scatter_dimension=1, tiled=True),
        lax.psum_scatter(grad_self_value, "dp", scatter_dimension=1, tiled=True),
        lax.psum_scatter(grad_self_out, "dp", scatter_dimension=1, tiled=True),
        lax.psum_scatter(grad_cross_query, "dp", scatter_dimension=1, tiled=True),
        lax.psum_scatter(grad_cross_key, "dp", scatter_dimension=1, tiled=True),
        lax.psum_scatter(grad_cross_value, "dp", scatter_dimension=1, tiled=True),
        lax.psum_scatter(grad_cross_out, "dp", scatter_dimension=1, tiled=True),
        lax.psum_scatter(grad_up, "dp", scatter_dimension=1, tiled=True),
        lax.psum_scatter(grad_down, "dp", scatter_dimension=1, tiled=True),
        lax.psum_scatter(norm_all, "dp", scatter_dimension=1, tiled=True),
    )
    return (
        output.reshape(row_count, length, width),
        text_grad.reshape(row_count, length, width),
        patch_grad,
        shares[0],
        shares[1],
        shares[2],
        shares[3],
        shares[4],
        shares[5],
        shares[6],
        shares[7],
        shares[8],
        shares[9],
        shares[10],
    )


def solution(mesh):
    in_specs = (
        P("dp", None, None),
        P("dp", None, None),
        P("dp", None),
        P("dp"),
        P(None, "dp"),
        P(None, "dp"),
        P(None, "dp"),
        P(None, "dp"),
        P(None, "dp"),
        P(None, "dp"),
        P(None, "dp"),
        P(None, "dp"),
        P(None, "dp"),
        P(None, "dp"),
        P(None, "dp"),
        P("dp", None, None),
    )
    out_specs = (
        P("dp", None, None),
        P("dp", None, None),
        P("dp", None, None),
        P(None, "dp"),
        P(None, "dp"),
        P(None, "dp"),
        P(None, "dp"),
        P(None, "dp"),
        P(None, "dp"),
        P(None, "dp"),
        P(None, "dp"),
        P(None, "dp"),
        P(None, "dp"),
        P(None, "dp"),
    )
    return jax.shard_map(local, mesh=mesh, in_specs=in_specs, out_specs=out_specs, check_vma=False)
```

profile of v0, /device:TPU:0, one launch (start us, length us, event | category | flops | bytes accessed | tf_op | source)
XLA Modules:
  0.0 1766.8 jit_solution(17364130538373085764)
XLA Ops:
  15.3 43.8 %all-gather = bf16[32,24,6]{1,2,0:T(8,128)(2,1)S(1)} all-gather(bf16[1,24,6]{1,2,0:T(8,128)(2,1)} %bitcast.107), channel_id=1, replica_groups=mesh['dp'=32] {'dp'}, dimensions={0}, use_global_device_ids=true | all-gather | bytes 9504 | tf_op jit(solution)/shard_map/all_gather | solution.py:127
  77.1 46.3 %all-gather.16.cloned.1.call-done = bf16[768,768]{0,1:T(8,128)(2,1)} async-done(((bf16[768,24]{0,1:T(8,128)(2,1)}), bf16[768,768]{0,1:T(8,128)(2,1)}) %all-gather.16.cloned.1.call-update) | async-done | bytes 1179664 | tf_op jit(solution)/shard_map/all_gather | solution.py:118
  130.6 48.6 %all-gather.12.cloned.1.call-done = bf16[768,768]{0,1:T(8,128)(2,1)} async-done(((bf16[768,24]{0,1:T(8,128)(2,1)}), bf16[768,768]{0,1:T(8,128)(2,1)}) %all-gather.12.cloned.1.call-update) | async-done | bytes 1179664 | tf_op jit(solution)/shard_map/all_gather | solution.py:119
  201.3 6.2 convert_element_type.144
  207.5 27.2 %all-gather.18.cloned.1.call-done = bf16[768,768]{0,1:T(8,128)(2,1)} async-done(((bf16[768,24]{0,1:T(8,128)(2,1)}), bf16[768,768]{0,1:T(8,128)(2,1)}) %all-gather.18.cloned.1.call-update) | async-done | bytes 1179664 | tf_op jit(solution)/shard_map/all_gather | solution.py:120
  238.9 51.4 %all-gather.22.cloned.1.call-done = bf16[768,768]{0,1:T(8,128)(2,1)} async-done(((bf16[768,24]{0,1:T(8,128)(2,1)}), bf16[768,768]{0,1:T(8,128)(2,1)}) %all-gather.22.cloned.1.call-update) | async-done | bytes 1179664 | tf_op jit(solution)/shard_map/all_gather | solution.py:121
  299.9 46.9 %all-gather.20.cloned.1.call-done = bf16[1024,768]{0,1:T(8,128)(2,1)} async-done(((bf16[1024,24]{0,1:T(8,128)(2,1)}), bf16[1024,768]{0,1:T(8,128)(2,1)}) %all-gather.20.cloned.1.call-update) | async-done | bytes 1572880 | tf_op jit(solution)/shard_map/all_gather | solution.py:123
  352.3 7.0 reshape.244
  359.4 11.3 copy.100
  370.7 32.9 %all-gather.24.cloned.1.call-done = bf16[1024,768]{0,1:T(8,128)(2,1)} async-done(((bf16[1024,24]{0,1:T(8,128)(2,1)}), bf16[1024,768]{0,1:T(8,128)(2,1)}) %all-gather.24.cloned.1.call-update) | async-done | bytes 1572880 | tf_op jit(solution)/shard_map/all_gather | solution.py:122
  409.0 7.0 reshape.245
  416.1 11.1 copy.102
  427.2 8.1 gather_fusion.1
  435.3 8.1 gather_fusion
  443.4 12.1 multiply_reduce_fusion.1
  455.5 8.4 fusion.13
  464.0 7.0 convert_bitcast_fusion.4
  484.5 40.4 %all-gather.28.cloned.1.call-done = bf16[768,3072]{0,1:T(8,128)(2,1)} async-done(((bf16[768,96]{0,1:T(8,128)(2,1)}), bf16[768,3072]{0,1:T(8,128)(2,1)}) %all-gather.28.cloned.1.call-update) | async-done | bytes 4718608 | tf_op jit(solution)/shard_map/all_gather | solution.py:125
  524.8 33.9 %multiply_convert_fusion.1 = (bf16[960,3072]{1,0:T(8,128)(2,1)}, f32[960,3072]{1,0:T(8,128)}, f32[960,3072]{1,0:T(8,128)}) fusion(bf16[768,3072]{0,1:T(8,128)(2,1)} %all-gather.28.cloned.1.call-done, f32[960,768]{1,0:T(8,128)S(1)} %get-tuple-element.44, f32[768]{0:T(1024)S(1)} %get-tuple-element.29, f32[768]{0:T(1024)S(1)} %get-tuple-element.30, ...), kind=kOutput, calls=%fused_computation.15 | convolution fusion | flops 4725227520 | bytes 37172736 | tf_op jit(solution)/shard_map/dot_general | solution.py:15
  558.7 30.8 %all-gather.30.cloned.1.call-done = bf16[3072,768]{0,1:T(8,128)(2,1)} async-done(((bf16[3072,24]{0,1:T(8,128)(2,1)}), bf16[3072,768]{0,1:T(8,128)(2,1)}) %all-gather.30.cloned.1.call-update) | async-done | bytes 4718608 | tf_op jit(solution)/shard_map/all_gather | solution.py:126
  589.6 9.3 fusion.134
  604.6 15.2 add_convert_fusion
  619.8 10.2 multiply_reduce_fusion.3
  646.9 11.4 fusion.39
  658.3 74.1 %convert_bitcast_fusion.3 = bf16[24,40,12,64]{3,1,2,0:T(8,128)(2,1)S(1)} fusion(f32[24,12,40,145]{3,2,1,0:T(8,128)} %fusion.39, f32[24,12,40,145]{3,2,1,0:T(8,128)} %get-tuple-element.42, f32[24,12,40]{2,1,0:T(8,128)S(1)} %log_add_fusion.1, bf16[24,145,12,64]{1,3,2,0:T(8,128)(2,1)} %gather_fusion.1, pred[24]{0:T(512)(128)(4,1)S(1)} %copy-done.50), kind=kOutput, calls=%fused_computation.79 | convolution fusion | flops 232266384 | bytes 20229144 | tf_op jit(solution)/shard_map/rhqk,rkhe->rqhe/dot_general | solution.py:83
  735.3 6.0 convert_element_type.163
  766.3 7.7 fusion.77
  774.0 14.2 convert_bitcast_fusion.2
  812.1 5.9 convert_element_type.176
  822.8 13.6 convert_bitcast_fusion.1
  851.9 80.6 %convolution_bitcast_fusion.1 = f32[24,145,12,64]{1,3,2,0:T(8,128)} fusion(f32[24,12,40,145]{3,2,1,0:T(8,128)} %fusion.39, f32[24,12,40,145]{3,2,1,0:T(8,128)} %get-tuple-element.42, f32[24,12,40]{2,1,0:T(8,128)S(1)} %log_add_fusion.1, bf16[24,40,12,64]{3,2,1,0:T(8,128)(2,1)} %reshape.208), kind=kOutput, calls=%fused_computation.36 | convolution fusion | flops 228856464 | bytes 25574400 | tf_op jit(solution)/shard_map/rhqk,rqhe->rkhe/dot_general | solution.py:86
  932.5 26.3 %fusion.41 = bf16[12,145,12,64]{1,0,3,2:T(8,128)(2,1)} fusion(f32[24,145,12,64]{1,3,2,0:T(8,128)} %convolution_bitcast_fusion.1, s32[24]{0:T(128)S(1)} %copy-done.48), kind=kOutput, calls=%fused_computation.58 | convolution fusion | flops 386196768 | bytes 13363296 | tf_op jit(solution)/shard_map/ri,rphe->iphe/dot_general | solution.py:228
  958.8 10.2 reshape.215
  969.1 7.6 convolution_bitcast_fusion.3
  976.8 12.0 convolution_bitcast_fusion
  988.8 25.9 %fusion.44 = bf16[12,145,12,64]{1,0,3,2:T(8,128)(2,1)} fusion(f32[24,145,12,64]{1,3,2,0:T(8,128)} %convolution_bitcast_fusion, s32[24]{0:T(128)S(1)} %copy-done.48), kind=kOutput, calls=%fused_computation.59 | convolution fusion | flops 386196768 | bytes 13363296 | tf_op jit(solution)/shard_map/ri,rphe->iphe/dot_general | solution.py:231
  1014.7 10.3 reshape.216
  1025.0 7.5 convolution_bitcast_fusion.2
  1033.2 10.9 fusion.122
  1044.1 10.7 fusion.95
  1066.3 8.7 reshape.217
  1075.0 39.5 %all-reduce = f32[6,768]{1,0:T(8,128)S(1)} all-reduce(f32[6,768]{1,0:T(8,128)S(1)} %concatenate.3), channel_id=12, replica_groups=mesh['dp'=32] {'dp'}, use_global_device_ids=true, to_apply=%region_34.36.clone | all-reduce | flops 4608 | bytes 36864
  1123.4 34.5 %reduce-scatter.16.cloned.1.call-done = f32[768,24]{0,1:T(8,128)} async-done(((f32[768,768]{0,1:T(8,128)}), f32[768,24]{0,1:T(8,128)}) %reduce-scatter.16.cloned.1.call-update) | async-done | bytes 73744 | tf_op jit(solution)/shard_map/reduce_scatter | solution.py:276
  1157.9 104.4 %reduce-scatter.14.cloned.1.call-done = f32[768,24]{0,1:T(8,128)} async-done(((f32[768,768]{0,1:T(8,128)}), f32[768,24]{0,1:T(8,128)}) %reduce-scatter.14.cloned.1.call-update) | async-done | bytes 73744 | tf_op jit(solution)/shard_map/reduce_scatter | solution.py:275
  1262.3 107.0 %reduce-scatter.22.cloned.1.call-done = f32[1024,24]{0,1:T(8,128)} async-done(((f32[1024,768]{0,1:T(8,128)}), f32[1024,24]{0,1:T(8,128)}) %reduce-scatter.22.cloned.1.call-update) | async-done | bytes 98320 | tf_op jit(solution)/shard_map/reduce_scatter | solution.py:279
  1369.3 107.1 %reduce-scatter.24.cloned.1.call-done = f32[1024,24]{0,1:T(8,128)} async-done(((f32[1024,768]{0,1:T(8,128)}), f32[1024,24]{0,1:T(8,128)}) %reduce-scatter.24.cloned.1.call-update) | async-done | bytes 98320 | tf_op jit(solution)/shard_map/reduce_scatter | solution.py:280
  1476.4 141.7 %reduce-scatter.28.cloned.1.call-done = f32[768,96]{0,1:T(8,128)} async-done(((f32[768,3072]{0,1:T(8,128)}), f32[768,96]{0,1:T(8,128)}) %reduce-scatter.28.cloned.1.call-update) | async-done | bytes 294928 | tf_op jit(solution)/shard_map/reduce_scatter | solution.py:282
  1618.1 141.5 %reduce-scatter.30.cloned.1.call-done = f32[3072,24]{0,1:T(8,128)} async-done(((f32[3072,768]{0,1:T(8,128)}), f32[3072,24]{0,1:T(8,128)}) %reduce-scatter.30.cloned.1.call-update) | async-done | bytes 294928 | tf_op jit(solution)/shard_map/reduce_scatter | solution.py:283
  (238 shorter events, 208.7 us)
Async XLA Ops:
  7.2 55.7 %copy-start.1 = (f32[24,40,768]{2,1,0:T(8,128)S(1)}, f32[24,40,768]{2,1,0:T(8,128)}, u32[]{:S(2)}) copy-start(f32[24,40,768]{2,1,0:T(8,128)} %param.33) | copy-start | bytes 8847364
  7.2 62.7 %all-gather.14.cloned.1.call-start = ((), (), s32[]{:S(2)}) async-start(), calls=%async_computation.11 | async-start | bytes 1216512 | tf_op jit(solution)/shard_map/all_gather | solution.py:117
  7.9 115.5 %all-gather.16.cloned.1.call-start = ((), (), s32[]{:S(2)}) async-start(), calls=%async_computation.12 | async-start | bytes 1216512 | tf_op jit(solution)/shard_map/all_gather | solution.py:118
  8.7 170.5 %all-gather.12.cloned.1.call-start = ((), (), s32[]{:S(2)}) async-start(), calls=%async_computation.10 | async-start | bytes 1216512 | tf_op jit(solution)/shard_map/all_gather | solution.py:119
  9.4 225.4 %all-gather.18.cloned.1.call-start = ((), (), s32[]{:S(2)}) async-start(), calls=%async_computation.13 | async-start | bytes 1216512 | tf_op jit(solution)/shard_map/all_gather | solution.py:120
  10.0 280.4 %all-gather.22.cloned.1.call-start = ((), (), s32[]{:S(2)}) async-start(), calls=%async_computation.15 | async-start | bytes 1216512 | tf_op jit(solution)/shard_map/all_gather | solution.py:121
  10.6 336.3 %all-gather.20.cloned.1.call-start = ((), (), s32[]{:S(2)}) async-start(), calls=%async_computation.14 | async-start | bytes 1622016 | tf_op jit(solution)/shard_map/all_gather | solution.py:123
  11.1 392.4 %all-gather.24.cloned.1.call-start = ((), (), s32[]{:S(2)}) async-start(), calls=%async_computation.16 | async-start | bytes 1622016 | tf_op jit(solution)/shard_map/all_gather | solution.py:122
  11.9 467.9 %all-gather.26.cloned.1.call-start = ((), (), s32[]{:S(2)}) async-start(), calls=%async_computation.17 | async-start | bytes 1216512 | tf_op jit(solution)/shard_map/all_gather | solution.py:124
  12.6 512.2 %all-gather.28.cloned.1.call-start = ((), (), s32[]{:S(2)}) async-start(), calls=%async_computation.18 | async-start | bytes 4866048 | tf_op jit(solution)/shard_map/all_gather | solution.py:125
  13.4 576.2 %all-gather.30.cloned.1.call-start = ((), (), s32[]{:S(2)}) async-start(), calls=%async_computation.19 | async-start | bytes 4866048 | tf_op jit(solution)/shard_map/all_gather | solution.py:126
  14.0 1109.4 %reduce-scatter.26.cloned.1.call-start = ((), (), s32[]{:S(2)}) async-start(), calls=%async_computation.27 | async-start | bytes 2433024 | tf_op jit(solution)/shard_map/reduce_scatter | solution.py:281
  14.7 449.3 %copy-start.49 = (pred[24]{0:T(512)(128)(4,1)}, pred[24]{0:T(512)(128)(4,1)S(1)}, u32[]{:S(2)}) copy-start(pred[24]{0:T(512)(128)(4,1)S(1)} %compare_and_fusion) | copy-start | bytes 76
  60.1 4.6 copy-start.28
  60.1 419.7 %copy-start.39 = (f32[768]{0:T(1024)}, f32[768]{0:T(1024)S(1)}, u32[]{:S(2)}) copy-start(f32[768]{0:T(1024)S(1)} %get-tuple-element.32) | copy-start | bytes 9220
  60.1 419.7 %copy-start.46 = (f32[768]{0:T(1024)}, f32[768]{0:T(1024)S(1)}, u32[]{:S(2)}) copy-start(f32[768]{0:T(1024)S(1)} %get-tuple-element.31) | copy-start | bytes 9220
  60.1 529.5 %copy-start.44 = (f32[768]{0:T(1024)}, f32[768]{0:T(1024)S(1)}, u32[]{:S(2)}) copy-start(f32[768]{0:T(1024)S(1)} %get-tuple-element.29) | copy-start | bytes 9220
  192.0 4.3 copy-start.4
  238.4 55.9 %copy-start.7 = (f32[960,768]{1,0:T(8,128)}, f32[960,768]{1,0:T(8,128)S(1)}, u32[]{:S(2)}) copy-start(f32[960,768]{1,0:T(8,128)S(1)} %get-tuple-element.40) | copy-start | bytes 8847364
  238.4 241.3 %copy-start.31 = (f32[960]{0:T(1024)}, f32[960]{0:T(1024)S(1)}, u32[]{:S(2)}) copy-start(f32[960]{0:T(1024)S(1)} %broadcast_multiply_fusion.8) | copy-start | bytes 11524
  238.9 240.9 %copy-start.37 = (f32[960]{0:T(1024)}, f32[960]{0:T(1024)S(1)}, u32[]{:S(2)}) copy-start(f32[960]{0:T(1024)S(1)} %add_rsqrt_fusion.2) | copy-start | bytes 11524
  455.5 8.4 copy-start.15
  455.5 8.5 copy-start
  464.0 7.1 copy-start.25
  484.0 146.1 %copy-start.6 = (f32[960,768]{1,0:T(8,128)}, f32[960,768]{1,0:T(8,128)S(1)}, u32[]{:S(2)}) copy-start(f32[960,768]{1,0:T(8,128)S(1)} %get-tuple-element.44) | copy-start | bytes 8847364
  589.6 9.8 copy-start.5
  600.7 3.9 slice-start
  604.6 15.2 copy-start.11
  635.6 487.8 %reduce-scatter.20.cloned.1.call-start = ((), (), s32[]{:S(2)}) async-start(), calls=%async_computation.24 | async-start | bytes 2433024 | tf_op jit(solution)/shard_map/reduce_scatter | solution.py:278
  641.1 5.8 copy-start.50
  735.3 6.0 copy-start.8
  735.3 6.0 copy-start.32
  735.3 6.0 copy-start.38
  735.3 6.0 copy-start.40
  735.3 6.0 copy-start.47
  745.9 377.5 %reduce-scatter.18.cloned.1.call-start = ((), (), s32[]{:S(2)}) async-start(), calls=%async_computation.23 | async-start | bytes 2433024 | tf_op jit(solution)/shard_map/reduce_scatter | solution.py:277
  746.3 5.5 copy-start.9
  756.2 367.2 %reduce-scatter.12.cloned.1.call-start = ((), (), s32[]{:S(2)}) async-start(), calls=%async_computation.20 | async-start | bytes 2433024 | tf_op jit(solution)/shard_map/reduce_scatter | solution.py:274
  766.3 7.7 copy-start.27
  803.5 354.4 %reduce-scatter.16.cloned.1.call-start = ((), (), s32[]{:S(2)}) async-start(), calls=%async_computation.22 | async-start | bytes 2433024 | tf_op jit(solution)/shard_map/reduce_scatter | solution.py:276
  822.7 439.6 %reduce-scatter.14.cloned.1.call-start = ((), (), s32[]{:S(2)}) async-start(), calls=%async_computation.21 | async-start | bytes 2433024 | tf_op jit(solution)/shard_map/reduce_scatter | solution.py:275
  851.6 80.9 %copy-start.48 = (s32[24]{0:T(128)S(1)}, s32[24]{0:T(128)}, u32[]{:S(2)}) copy-start(s32[24]{0:T(128)} %param.21) | copy-start | bytes 292
  851.6 517.7 %reduce-scatter.22.cloned.1.call-start = ((), (), s32[]{:S(2)}) async-start(), calls=%async_computation.25 | async-start | bytes 3244032 | tf_op jit(solution)/shard_map/reduce_scatter | solution.py:279
  976.8 499.6 %reduce-scatter.24.cloned.1.call-start = ((), (), s32[]{:S(2)}) async-start(), calls=%async_computation.26 | async-start | bytes 3244032 | tf_op jit(solution)/shard_map/reduce_scatter | solution.py:280
  1032.5 585.6 %reduce-scatter.28.cloned.1.call-start = ((), (), s32[]{:S(2)}) async-start(), calls=%async_computation.28 | async-start | bytes 9732096 | tf_op jit(solution)/shard_map/reduce_scatter | solution.py:282
  1044.1 715.5 %reduce-scatter.30.cloned.1.call-start = ((), (), s32[]{:S(2)}) async-start(), calls=%async_computation.29 | async-start | bytes 9732096 | tf_op jit(solution)/shard_map/reduce_scatter | solution.py:283
  1055.5 5.4 copy-start.14
  1055.6 5.4 copy-start.51
  (27 other events, 52.8 us)
Sparse Core Ops, SparseCore 0:
  10.9 56.6 all-gather.13
  70.5 52.8 all-gather.15
  126.3 52.8 all-gather.11
  181.9 52.8 all-gather.17
  237.5 52.8 all-gather.21
  293.1 53.6 all-gather.19
  349.7 53.8 all-gather.23
  406.4 52.9 all-gather.25
  462.3 62.4 all-gather.27
  527.6 61.9 all-gather.29
  635.7 98.1 reduce-scatter.25
  746.0 97.9 reduce-scatter.19
  849.8 98.8 reduce-scatter.17
  954.4 98.7 reduce-scatter.11
  1058.9 98.9 reduce-scatter.15
  1163.6 98.6 reduce-scatter.13
  1268.1 101.1 reduce-scatter.21
  1375.2 101.1 reduce-scatter.23
  1482.9 135.2 reduce-scatter.27
  1624.4 135.1 reduce-scatter.29
where the time goes:
time: 1780 us; the launch traced here: 1770 us
  waiting for transfers between devices  967 us (54%)
  matrix products  491 us (28%)
  local copies, waits for them, and re-layouts  184 us (10%)
  blocking collectives  83.3 us (5%)
  other arithmetic  24.5 us (1%)
    reduce_scatter x1, waiting for transfers between devices, local(): lax.psum_scatter(grad_up, 'dp', scatter_dimension=1, tiled=True)  142 us
    reduce_scatter x1, waiting for transfers between devices, local(): lax.psum_scatter(grad_down, 'dp', scatter_dimension=1, tiled=True)  141 us
    reduce_scatter x1, waiting for transfers between devices, local(): lax.psum_scatter(grad_cross_value, 'dp', scatter_dimension=1, tiled=True)  107 us
    reduce_scatter x1, waiting for transfers between devices, local(): lax.psum_scatter(grad_cross_key, 'dp', scatter_dimension=1, tiled=True)  107 us
    reduce_scatter x1, waiting for transfers between devices, local(): lax.psum_scatter(grad_self_key, 'dp', scatter_dimension=1, tiled=True)  104 us
    dot_general x2, matrix products, attend_back(): jnp.einsum('rhqk,rqhe->rkhe', grad_scores, queries, preferred_element_typ...  94.2 us
    dot_general x2, matrix products, attend_back(): jnp.einsum('rhqk,rkhe->rqhe', grad_scores, key_rows, preferred_element_ty...  88.3 us
    dot_general x10, matrix products, project(): return jnp.dot(left, right, preferred_element_type=jnp.float32)  75 us
  transfers between devices with their start and end apart: 20, of which 14 were waited for; matrix products, arithmetic and copies ran while one was open for 37% of the time, Pallas kernels for 0%

commit v1 on v0

v1 whole, which is shorter than its diff:
```python
import functools

import jax
import jax.numpy as jnp
from jax import lax
from jax.experimental import pallas as pl
from jax.experimental.pallas import tpu as pltpu
from jax.sharding import PartitionSpec as P

HEADS = 12
HD = 64
LANES = 128
PAIRS = HEADS // 2
ROWS_BLOCK = 6
GROUP = 2
PATCH_PAD = 160
IMAGE_BLOCK = 4
VMEM_BYTES = 66_000_000
MASKED = -1e30
EPSILON = 1e-06
F32 = jnp.float32
BF16 = jnp.bfloat16


def nt(left, right):
    return lax.dot_general(left, right, (((1,), (1,)), ((), ())), preferred_element_type=F32)


def nn(left, right):
    return lax.dot_general(left, right, (((1,), (0,)), ((), ())), preferred_element_type=F32)


def tn(left, right):
    return lax.dot_general(left, right, (((0,), (0,)), ((), ())), preferred_element_type=F32)


def normalize(residual):
    average = jnp.mean(residual, axis=-1, keepdims=True)
    centered = residual - average
    inverse = lax.rsqrt(jnp.mean(centered * centered, axis=-1, keepdims=True) + EPSILON)
    return centered * inverse, inverse


def normalize_back(grad, normed, inverse, gain):
    scaled = grad * gain
    return inverse * (
        scaled
        - jnp.mean(scaled, axis=-1, keepdims=True)
        - normed * jnp.mean(scaled * normed, axis=-1, keepdims=True)
    )


def half_masks(dtype, scale=1.0):
    lane = lax.broadcasted_iota(jnp.int32, (1, LANES), 1)
    low = jnp.where(lane < HD, scale, 0.0)
    high = jnp.where(lane < HD, 0.0, scale)
    return low.astype(dtype), high.astype(dtype)


def merge_halves(stacked):
    half = stacked.shape[0] // 2
    lane = lax.broadcasted_iota(jnp.int32, (half, LANES), 1)
    return jnp.where(lane < HD, stacked[:half], stacked[half:])


def softmax(scores):
    exponent = jnp.exp(scores - jnp.max(scores, axis=-1, keepdims=True))
    return (exponent * (1.0 / jnp.sum(exponent, axis=-1, keepdims=True))).astype(BF16)


def images_kernel(patches_ref, key_ref, value_ref, padded_ref, keys_ref, values_ref):
    images, patches, width = patches_ref.shape
    tail = PATCH_PAD - 16
    for image in range(images):
        padded_ref[image, tail:, :] = jnp.zeros((PATCH_PAD - tail, width), BF16)
        padded_ref[image, :patches, :] = patches_ref[image]
    rows = padded_ref[...].reshape(images * PATCH_PAD, width)
    shape = (images, PATCH_PAD, key_ref.shape[0])
    keys_ref[...] = nt(rows, key_ref[...]).astype(BF16).reshape(shape)
    values_ref[...] = nt(rows, value_ref[...]).astype(BF16).reshape(shape)


def whole(shape):
    return pl.BlockSpec(shape, lambda *_: (0,) * len(shape), pipeline_mode=pl.Buffered(1))


def image_rows(patches, cross_key, cross_value):
    images, count, width = patches.shape
    inner = cross_key.shape[0]

    def block(middle, last):
        return pl.BlockSpec((IMAGE_BLOCK, middle, last), lambda i: (i, 0, 0))

    return pl.pallas_call(
        images_kernel,
        grid=(images // IMAGE_BLOCK,),
        in_specs=[block(count, width), whole(cross_key.shape), whole(cross_value.shape)],
        out_specs=[block(PATCH_PAD, width), block(PATCH_PAD, inner), block(PATCH_PAD, inner)],
        out_shape=[
            jax.ShapeDtypeStruct((images, PATCH_PAD, width), BF16),
            jax.ShapeDtypeStruct((images, PATCH_PAD, inner), BF16),
            jax.ShapeDtypeStruct((images, PATCH_PAD, inner), BF16),
        ],
        compiler_params=pltpu.CompilerParams(vmem_limit_bytes=VMEM_BYTES),
        name="image_rows",
    )(patches, cross_key, cross_value)


def patch_kernel(keys_ref, values_ref, key_ref, value_ref, out_ref):
    images, count, width = out_ref.shape
    grad = nn(keys_ref[...].reshape(-1, key_ref.shape[0]), key_ref[...])
    grad += nn(values_ref[...].reshape(-1, key_ref.shape[0]), value_ref[...])
    grad = grad.reshape(images, PATCH_PAD, width)
    for image in range(images):
        out_ref[image] = grad[image, :count]


def patch_grads(grad_keys, grad_values, cross_key, cross_value, count):
    images, _, inner = grad_keys.shape
    width = cross_key.shape[1]
    block = pl.BlockSpec((IMAGE_BLOCK, PATCH_PAD, inner), lambda i: (i, 0, 0))
    return pl.pallas_call(
        patch_kernel,
        grid=(images // IMAGE_BLOCK,),
        in_specs=[block, block, whole(cross_key.shape), whole(cross_value.shape)],
        out_specs=pl.BlockSpec((IMAGE_BLOCK, count, width), lambda i: (i, 0, 0)),
        out_shape=jax.ShapeDtypeStruct((images, count, width), F32),
        compiler_params=pltpu.CompilerParams(vmem_limit_bytes=VMEM_BYTES),
        name="patch_grads",
    )(grad_keys, grad_values, cross_key, cross_value)


def forward_kernel(
    patch_count,
    image_ref,
    text_ref,
    id_column_ref,
    id_row_ref,
    cotangent_ref,
    keys_ref,
    values_ref,
    query_ref,
    key_ref,
    value_ref,
    out_proj_ref,
    cross_query_ref,
    cross_out_ref,
    up_ref,
    down_ref,
    norm_ref,
    output_ref,
    qkv_ref,
    self_weights_ref,
    mixed_self_ref,
    normed_one_ref,
    inverse_one_ref,
    first_low_ref,
    cross_low_ref,
    cross_weights_ref,
    mixed_cross_ref,
    second_low_ref,
    hidden_ref,
    grad_pre_ref,
    branch_three_ref,
    grad_two_ref,
    norm_grad_ref,
    cross_wide,
    mixed_wide,
    slope,
):
    step = pl.program_id(0)
    length = text_ref.shape[0] // ROWS_BLOCK
    width = text_ref.shape[1]
    tokens = text_ref[...]
    for index, weight in enumerate((query_ref, key_ref, value_ref)):
        qkv_ref[:, index * width : (index + 1) * width] = nt(tokens, weight[...]).astype(BF16)

    low, high = half_masks(BF16, 0.125)
    size = GROUP * length
    for group in range(ROWS_BLOCK // GROUP):
        rows = slice(group * size, (group + 1) * size)
        same = id_column_ref[rows, :] == id_row_ref[0, group : group + 1, :]
        bias = jnp.where(same, 0.0, MASKED)
        bias = jnp.concatenate([bias, bias], axis=0)
        for pair in range(PAIRS):
            at = pair * LANES
            queries = qkv_ref[rows, at : at + LANES]
            stacked = jnp.concatenate([queries * low, queries * high], axis=0)
            scores = nt(stacked, qkv_ref[rows, width + at : width + at + LANES]) + bias
            weights = softmax(scores)
            self_weights_ref[group, pair] = weights
            mixed = nn(weights, qkv_ref[rows, 2 * width + at : 2 * width + at + LANES])
            mixed_self_ref[rows, at : at + LANES] = merge_halves(mixed).astype(BF16)

    normed_one, inverse_one = normalize(
        tokens.astype(F32) + nt(mixed_self_ref[...], out_proj_ref[...])
    )
    normed_one_ref[...] = normed_one
    inverse_one_ref[...] = inverse_one
    first = normed_one * norm_ref[0:1, :] + norm_ref[1:2, :]
    first_low_ref[...] = first.astype(BF16)
    cross_low = nt(first_low_ref[...], cross_query_ref[...]).astype(BF16)
    cross_low_ref[...] = cross_low
    cross_wide[...] = cross_low.astype(F32)

    low_wide, high_wide = half_masks(F32, 0.125)
    column = lax.broadcasted_iota(jnp.int32, (1, PATCH_PAD), 1)
    tail = jnp.where(column < patch_count, 0.0, MASKED)
    for row in range(ROWS_BLOCK):
        rows = slice(row * length, (row + 1) * length)
        image = image_ref[step * ROWS_BLOCK + row]
        for pair in range(PAIRS):
            at = pair * LANES
            queries = cross_wide[rows, at : at + LANES]
            stacked = jnp.concatenate([queries * low_wide, queries * high_wide], axis=0)
            scores = nt(stacked.astype(BF16), keys_ref[image, :, at : at + LANES]) + tail
            weights = softmax(scores)
            cross_weights_ref[row, pair] = weights
            mixed = nn(weights, values_ref[image, :, at : at + LANES])
            mixed_wide[rows, at : at + LANES] = merge_halves(mixed)
    mixed_cross_ref[...] = mixed_wide[...].astype(BF16)

    normed_two, inverse_two = normalize(first + nt(mixed_cross_ref[...], cross_out_ref[...]))
    second = normed_two * norm_ref[2:3, :] + norm_ref[3:4, :]
    second_low_ref[...] = second.astype(BF16)

    total = second
    for start in range(0, hidden_ref.shape[1], width):
        part = slice(start, start + width)
        pre = nt(second_low_ref[...], up_ref[part, :])
        gate = 0.5 + 0.5 * lax.erf(pre * 0.7071067811865476)
        slope[:, part] = (
            gate + pre * (0.3989422804014327 * jnp.exp(-0.5 * pre * pre))
        ).astype(BF16)
        hidden = (pre * gate).astype(BF16)
        hidden_ref[:, part] = hidden
        total += nt(hidden, down_ref[:, part])

    normed_three, inverse_three = normalize(total)
    output_ref[...] = normed_three * norm_ref[4:5, :] + norm_ref[5:6, :]
    grad = cotangent_ref[...]
    terms = [
        None,
        None,
        None,
        None,
        jnp.sum(grad * normed_three, axis=0, keepdims=True),
        jnp.sum(grad, axis=0, keepdims=True),
    ]
    grad_three = normalize_back(grad, normed_three, inverse_three, norm_ref[4:5, :])
    branch_three = grad_three.astype(BF16)
    branch_three_ref[...] = branch_three
    grad_second = grad_three
    for start in range(0, hidden_ref.shape[1], width):
        part = slice(start, start + width)
        grad_pre = (nn(branch_three, down_ref[:, part]) * slope[:, part].astype(F32)).astype(BF16)
        grad_pre_ref[:, part] = grad_pre
        grad_second += nn(grad_pre, up_ref[part, :])
    terms[2] = jnp.sum(grad_second * normed_two, axis=0, keepdims=True)
    terms[3] = jnp.sum(grad_second, axis=0, keepdims=True)
    grad_two_ref[...] = normalize_back(grad_second, normed_two, inverse_two, norm_ref[2:3, :])

    @pl.when(step == 0)
    def _():
        norm_grad_ref[...] = jnp.zeros_like(norm_grad_ref)

    for index in range(2, 6):
        norm_grad_ref[index : index + 1, :] += terms[index]


def forward(row_image, text, ids, cotangent, keys, values, weights, norms, patch_count):
    rows, length, width = text.shape
    hidden = weights["up"].shape[0]
    size = ROWS_BLOCK * length
    count = rows * length
    groups = ROWS_BLOCK // GROUP
    steps = rows // ROWS_BLOCK

    def tokens(last):
        return pl.BlockSpec((size, last), lambda i, *_: (i, 0))

    def units(number, left, right):
        return pl.BlockSpec((number, PAIRS, left, right), lambda i, *_: (i, 0, 0, 0))

    names = ("query", "key", "value", "out", "cross_query", "cross_out", "up", "down")
    held = [weights[name] for name in names]
    pair_rows = 2 * length
    stack_rows = 2 * GROUP * length
    outs = [
        ((count, width), F32, tokens(width)),
        ((count, 3 * width), BF16, tokens(3 * width)),
        (
            (rows // GROUP, PAIRS, stack_rows, GROUP * length),
            BF16,
            units(groups, stack_rows, GROUP * length),
        ),
        ((count, width), BF16, tokens(width)),
        ((count, width), F32, tokens(width)),
        ((count, 1), F32, tokens(1)),
        ((count, width), BF16, tokens(width)),
        ((count, width), BF16, tokens(width)),
        ((rows, PAIRS, pair_rows, PATCH_PAD), BF16, units(ROWS_BLOCK, pair_rows, PATCH_PAD)),
        ((count, width), BF16, tokens(width)),
        ((count, width), BF16, tokens(width)),
        ((count, hidden), BF16, tokens(hidden)),
        ((count, hidden), BF16, tokens(hidden)),
        ((count, width), BF16, tokens(width)),
        ((count, width), F32, tokens(width)),
        ((8, width), F32, pl.BlockSpec((8, width), lambda i, *_: (0, 0))),
    ]
    return pl.pallas_call(
        functools.partial(forward_kernel, patch_count),
        grid_spec=pltpu.PrefetchScalarGridSpec(
            num_scalar_prefetch=1,
            grid=(steps,),
            in_specs=[
                tokens(width),
                tokens(1),
                pl.BlockSpec((1, groups, GROUP * length), lambda i, *_: (i, 0, 0)),
                tokens(width),
                whole(keys.shape),
                whole(values.shape),
                *[whole(array.shape) for array in held],
                whole(norms.shape),
            ],
            out_specs=[spec for _, _, spec in outs],
            scratch_shapes=[
                pltpu.VMEM((size, width), F32),
                pltpu.VMEM((size, width), F32),
                pltpu.VMEM((size, hidden), BF16),
            ],
        ),
        out_shape=[jax.ShapeDtypeStruct(shape, dtype) for shape, dtype, _ in outs],
        compiler_params=pltpu.CompilerParams(vmem_limit_bytes=VMEM_BYTES),
        name="forward",
    )(
        row_image,
        text.reshape(count, width),
        ids.reshape(count, 1),
        ids.reshape(steps, groups, GROUP * length),
        cotangent.reshape(count, width),
        keys,
        values,
        *held,
        norms,
    )


def backward_kernel(
    image_ref,
    grad_two_ref,
    qkv_ref,
    self_weights_ref,
    normed_one_ref,
    inverse_one_ref,
    cross_low_ref,
    cross_weights_ref,
    keys_ref,
    values_ref,
    query_ref,
    key_ref,
    value_ref,
    out_proj_ref,
    cross_query_ref,
    cross_out_ref,
    norm_ref,
    text_grad_ref,
    branch_two_ref,
    grad_cross_ref,
    branch_one_ref,
    grad_qkv_ref,
    grad_keys_ref,
    grad_values_ref,
    norm_grad_ref,
    cross_wide,
    mixed_wide,
    grad_wide,
    grad_mixed,
    key_total,
    value_total,
):
    step = pl.program_id(0)
    length = grad_two_ref.shape[0] // ROWS_BLOCK
    width = grad_two_ref.shape[1]

    @pl.when(step == 0)
    def _():
        norm_grad_ref[...] = jnp.zeros_like(norm_grad_ref)
        key_total[...] = jnp.zeros_like(key_total)
        value_total[...] = jnp.zeros_like(value_total)

    grad_two = grad_two_ref[...]
    branch_two = grad_two.astype(BF16)
    branch_two_ref[...] = branch_two
    mixed_wide[...] = nn(branch_two, cross_out_ref[...])
    cross_wide[...] = cross_low_ref[...].astype(F32)
    low_wide, high_wide = half_masks(F32)
    for row in range(ROWS_BLOCK):
        rows = slice(row * length, (row + 1) * length)
        image = image_ref[step * ROWS_BLOCK + row]
        for pair in range(PAIRS):
            lanes = slice(pair * LANES, (pair + 1) * LANES)
            queries = cross_wide[rows, lanes]
            queries = jnp.concatenate([queries * low_wide, queries * high_wide], axis=0).astype(BF16)
            mixed = mixed_wide[rows, lanes]
            mixed = jnp.concatenate([mixed * low_wide, mixed * high_wide], axis=0).astype(BF16)
            weights_low = cross_weights_ref[row, pair]
            weights = weights_low.astype(F32)
            grad_weights = nt(mixed, values_ref[image, :, lanes])
            inner = jnp.sum(grad_weights * weights, axis=-1, keepdims=True)
            grad_scores = (weights * (grad_weights - inner) * 0.125).astype(BF16)
            grad_wide[rows, lanes] = merge_halves(nn(grad_scores, keys_ref[image, :, lanes]))
            key_total[image, :, lanes] += tn(grad_scores, queries)
            value_total[image, :, lanes] += tn(weights_low, mixed)
    grad_cross = grad_wide[...].astype(BF16)
    grad_cross_ref[...] = grad_cross

    grad_first = grad_two + nn(grad_cross, cross_query_ref[...])
    normed_one = normed_one_ref[...]
    norm_grad_ref[0:1, :] += jnp.sum(grad_first * normed_one, axis=0, keepdims=True)
    norm_grad_ref[1:2, :] += jnp.sum(grad_first, axis=0, keepdims=True)
    grad_one = normalize_back(grad_first, normed_one, inverse_one_ref[...], norm_ref[0:1, :])
    branch_one = grad_one.astype(BF16)
    branch_one_ref[...] = branch_one
    grad_mixed[...] = nn(branch_one, out_proj_ref[...]).astype(BF16)

    low, high = half_masks(BF16)
    size = GROUP * length
    for group in range(ROWS_BLOCK // GROUP):
        rows = slice(group * size, (group + 1) * size)
        for pair in range(PAIRS):
            at = pair * LANES
            queries = qkv_ref[rows, at : at + LANES]
            queries = jnp.concatenate([queries * low, queries * high], axis=0)
            keys = qkv_ref[rows, width + at : width + at + LANES]
            values = qkv_ref[rows, 2 * width + at : 2 * width + at + LANES]
            mixed = grad_mixed[rows, at : at + LANES]
            mixed = jnp.concatenate([mixed * low, mixed * high], axis=0)
            weights_low = self_weights_ref[group, pair]
            weights = weights_low.astype(F32)
            grad_weights = nt(mixed, values)
            inner = jnp.sum(grad_weights * weights, axis=-1, keepdims=True)
            grad_scores = (weights * (grad_weights - inner) * 0.125).astype(BF16)
            grad_qkv_ref[rows, at : at + LANES] = merge_halves(nn(grad_scores, keys)).astype(BF16)
            at += width
            grad_qkv_ref[rows, at : at + LANES] = tn(grad_scores, queries).astype(BF16)
            at += width
            grad_qkv_ref[rows, at : at + LANES] = tn(weights_low, mixed).astype(BF16)

    text_grad = grad_one
    for index, weight in enumerate((query_ref, key_ref, value_ref)):
        text_grad += nn(grad_qkv_ref[:, index * width : (index + 1) * width], weight[...])
    text_grad_ref[...] = text_grad

    @pl.when(step == pl.num_programs(0) - 1)
    def _():
        grad_keys_ref[...] = key_total[...].astype(BF16)
        grad_values_ref[...] = value_total[...].astype(BF16)


def backward(row_image, saved, keys, values, weights, norms, rows):
    grad_two, qkv, self_weights, normed_one, inverse_one, cross_low, cross_weights = saved
    count, width = grad_two.shape
    length = count // rows
    size = ROWS_BLOCK * length
    groups = ROWS_BLOCK // GROUP

    def tokens(last):
        return pl.BlockSpec((size, last), lambda i, *_: (i, 0))

    def units(number, left, right):
        return pl.BlockSpec((number, PAIRS, left, right), lambda i, *_: (i, 0, 0, 0))

    names = ("query", "key", "value", "out", "cross_query", "cross_out")
    held = [weights[name] for name in names]
    low = jax.ShapeDtypeStruct((count, width), BF16)
    images = jax.ShapeDtypeStruct(keys.shape, BF16)
    return pl.pallas_call(
        backward_kernel,
        grid_spec=pltpu.PrefetchScalarGridSpec(
            num_scalar_prefetch=1,
            grid=(rows // ROWS_BLOCK,),
            in_specs=[
                tokens(width),
                tokens(3 * width),
                units(groups, 2 * GROUP * length, GROUP * length),
                tokens(width),
                tokens(1),
                tokens(width),
                units(ROWS_BLOCK, 2 * length, PATCH_PAD),
                whole(keys.shape),
                whole(values.shape),
                *[whole(array.shape) for array in held],
                whole(norms.shape),
            ],
            out_specs=[
                tokens(width),
                tokens(width),
                tokens(width),
                tokens(width),
                tokens(3 * width),
                whole(keys.shape),
                whole(keys.shape),
                pl.BlockSpec((8, width), lambda i, *_: (0, 0)),
            ],
            scratch_shapes=[
                pltpu.VMEM((size, width), F32),
                pltpu.VMEM((size, width), F32),
                pltpu.VMEM((size, width), F32),
                pltpu.VMEM((size, width), BF16),
                pltpu.VMEM(keys.shape, F32),
                pltpu.VMEM(keys.shape, F32),
            ],
        ),
        out_shape=[
            jax.ShapeDtypeStruct((count, width), F32),
            low,
            low,
            low,
            jax.ShapeDtypeStruct((count, 3 * width), BF16),
            images,
            images,
            jax.ShapeDtypeStruct((8, width), F32),
        ],
        compiler_params=pltpu.CompilerParams(vmem_limit_bytes=VMEM_BYTES),
        name="backward",
    )(row_image, grad_two, qkv, self_weights, normed_one, inverse_one, cross_low, cross_weights, keys, values, *held, norms)


NAMES = (
    "query",
    "key",
    "value",
    "out",
    "cross_query",
    "cross_key",
    "cross_value",
    "cross_out",
    "up",
    "down",
)


def gather(shards, norm):
    full = {name: lax.all_gather(shards[name], "dp", axis=0, tiled=True) for name in NAMES}
    return full, lax.all_gather(norm, "dp", axis=1, tiled=True)


def local(text, patches, segment_ids, row_image, *rest):
    *shards, norm_params, cotangent = rest
    shards = {name: jnp.swapaxes(shard, 0, 1) for name, shard in zip(NAMES, shards, strict=True)}
    rows, length, width = text.shape
    weights, norms = gather(shards, norm_params)
    norms = norms.astype(F32)
    norms = jnp.concatenate([norms, jnp.zeros((2, width), F32)], axis=0)
    ids = segment_ids + 8 * jnp.arange(rows, dtype=jnp.int32)[:, None]
    padded, keys, values = image_rows(patches, weights["cross_key"], weights["cross_value"])
    (
        output,
        qkv,
        self_weights,
        mixed_self,
        normed_one,
        inverse_one,
        first_low,
        cross_low,
        cross_weights,
        mixed_cross,
        second_low,
        hidden,
        grad_pre,
        branch_three,
        grad_two,
        norm_late,
    ) = forward(
        row_image, text, ids, cotangent, keys, values, weights, norms, patches.shape[1]
    )
    (
        text_grad,
        branch_two,
        grad_cross,
        branch_one,
        grad_qkv,
        grad_keys,
        grad_values,
        norm_early,
    ) = backward(
        row_image,
        (grad_two, qkv, self_weights, normed_one, inverse_one, cross_low, cross_weights),
        keys,
        values,
        weights,
        norms,
        rows,
    )
    patch_grad = patch_grads(
        grad_keys, grad_values, weights["cross_key"], weights["cross_value"], patches.shape[1]
    )
    tokens = text.reshape(rows * length, width)
    patch_rows = padded.reshape(-1, padded.shape[-1])
    products = (
        (grad_qkv[:, :width], tokens),
        (grad_qkv[:, width : 2 * width], tokens),
        (grad_qkv[:, 2 * width :], tokens),
        (branch_one, mixed_self),
        (grad_cross, first_low),
        (grad_keys.reshape(-1, width), patch_rows),
        (grad_values.reshape(-1, width), patch_rows),
        (branch_two, mixed_cross),
        (grad_pre, second_low),
        (branch_three, hidden),
    )
    grads = []
    for left, right in products:
        grad = tn(left, right).astype(BF16)
        grads.append(lax.psum_scatter(grad, "dp", scatter_dimension=0, tiled=True))
    norm_grad = lax.psum_scatter(
        (norm_late + norm_early)[:6], "dp", scatter_dimension=1, tiled=True
    )
    return (
        output.reshape(text.shape),
        text_grad.reshape(text.shape),
        patch_grad,
        *[jnp.swapaxes(grad, 0, 1).astype(F32) for grad in grads],
        norm_grad,
    )


def solution(mesh):
    split = P("dp", None, None)
    columns = P(None, "dp")
    in_specs = (split, split, P("dp", None), P("dp"), *([columns] * 11), split)
    out_specs = (split, split, split, *([columns] * 11))
    return jax.shard_map(local, mesh=mesh, in_specs=in_specs, out_specs=out_specs, check_vma=False)
```

time: 1780 us -> 1830 us (1.028)
  waiting for transfers between devices: 967 us -> 1430 us
  matrix products: 491 us -> 58 us
  Pallas kernels: 0 us -> 212 us
  local copies, waits for them, and re-layouts: 184 us -> 5.08 us
    dot_general x44 -> x10, matrix products: 491 us -> 58 us  [tn(): lax.dot_general(left, right, (((0,), (0,)), ((), ())), preferred_element_...]
    reduce_scatter x10, waiting for transfers between devices: 636 us -> 908 us  [local(): grads.append(lax.psum_scatter(grad, 'dp', scatter_dimension=0, tiled=True))]
    pallas_call x0 -> x4, Pallas kernels: none -> 212 us  [the longest x1 104 us: forward(): pl.pallas_call(functools.partial(forward_kernel, patch_count), grid_spec=...]
    all_gather x10, waiting for transfers between devices: 324 us -> 518 us  [gather(): lax.all_gather(shards[name], 'dp', axis=0, tiled=True)]
    reshape x14 -> x2, local copies, waits for them, and re-layouts: 99.4 us -> 1.65 us  [the longest x1 0.97 us: forward(): ids.reshape(count, 1)]
    convert_element_type x14 -> x0, local copies, waits for them, and re-layouts: 56.6 us -> none  [the longest x2 10.6 us: local(): grad_query_low = grad_query_self.reshape(-1, width).astype(jnp.bfloat16)]
  transfers between devices with their start and end apart: 20 -> 20, of which waited for: 14 -> 19; matrix products, arithmetic and copies ran while one was open for 37% -> 4% of each run, Pallas kernels for 0% -> 1%
where the time goes in v1:
time: 1830 us; the launch traced here: 1820 us
  waiting for transfers between devices  1430 us (78%)
  Pallas kernels  212 us (12%)
  blocking collectives  83.2 us (5%)
  matrix products  58 us (3%)
    reduce_scatter x10, waiting for transfers between devices, local(): grads.append(lax.psum_scatter(grad, 'dp', scatter_dimension=0, tiled=True))  908 us
    all_gather x10, waiting for transfers between devices, gather(): lax.all_gather(shards[name], 'dp', axis=0, tiled=True)  518 us
    pallas_call x1, Pallas kernels, forward(): pl.pallas_call(functools.partial(forward_kernel, patch_count), grid_spec=...  104 us
    pallas_call x1, Pallas kernels, backward(): pl.pallas_call(backward_kernel, grid_spec=pltpu.PrefetchScalarGridSpec(nu...  86.8 us
    dot_general x10, matrix products, tn(): lax.dot_general(left, right, (((0,), (0,)), ((), ())), preferred_element_...  58 us
    all_gather x1, blocking collectives, gather(): return (full, lax.all_gather(norm, 'dp', axis=1, tiled=True))  43.9 us
    unnamed x1, blocking collectives  39.3 us
  transfers between devices with their start and end apart: 20, of which 19 were waited for; matrix products, arithmetic and copies ran while one was open for 4% of the time, Pallas kernels for 1%

profile of v1, /device:TPU:0, one launch (start us, length us, event | category | flops | bytes accessed | tf_op | source)
XLA Modules:
  0.0 1822.4 jit_solution(707170184706361716)
XLA Ops:
  15.5 1.0 reshape.65.id_column_ref
  16.4 43.9 %all-gather = bf16[32,24,6]{1,2,0:T(8,128)(2,1)S(1)} all-gather(bf16[1,24,6]{1,2,0:T(8,128)(2,1)} %bitcast.79), channel_id=1, replica_groups=mesh['dp'=32] {'dp'}, dimensions={0}, use_global_device_ids=true | all-gather | bytes 9504 | tf_op jit(solution)/shard_map/all_gather | solution.py:546
  61.1 7.4 all-gather.12.cloned.1.call-done.key_ref
  68.5 56.7 %all-gather.14.cloned.1.call-done.value_ref = bf16[768,1024]{1,0:T(8,128)(2,1)} async-done(((bf16[24,1024]{1,0:T(8,128)(2,1)}), bf16[768,1024]{1,0:T(8,128)(2,1)}) %all-gather.14.cloned.1.call-update) | async-done | bytes 1572880 | tf_op jit(solution)/shard_map/all_gather | solution.py:545
  125.2 10.1 image_rows.1
  135.3 45.8 %all-gather.16.cloned.1.call-done.query_ref = bf16[768,768]{1,0:T(8,128)(2,1)} async-done(((bf16[24,768]{1,0:T(8,128)(2,1)}), bf16[768,768]{1,0:T(8,128)(2,1)}) %all-gather.16.cloned.1.call-update) | async-done | bytes 1179664 | tf_op jit(solution)/shard_map/all_gather | solution.py:545
  181.1 55.6 %all-gather.18.cloned.1.call-done.key_ref = bf16[768,768]{1,0:T(8,128)(2,1)} async-done(((bf16[24,768]{1,0:T(8,128)(2,1)}), bf16[768,768]{1,0:T(8,128)(2,1)}) %all-gather.18.cloned.1.call-update) | async-done | bytes 1179664 | tf_op jit(solution)/shard_map/all_gather | solution.py:545
  236.7 55.6 %all-gather.20.cloned.1.call-done.value_ref = bf16[768,768]{1,0:T(8,128)(2,1)} async-done(((bf16[24,768]{1,0:T(8,128)(2,1)}), bf16[768,768]{1,0:T(8,128)(2,1)}) %all-gather.20.cloned.1.call-update) | async-done | bytes 1179664 | tf_op jit(solution)/shard_map/all_gather | solution.py:545
  292.3 55.6 %all-gather.22.cloned.1.call-done.out_proj_ref = bf16[768,768]{1,0:T(8,128)(2,1)} async-done(((bf16[24,768]{1,0:T(8,128)(2,1)}), bf16[768,768]{1,0:T(8,128)(2,1)}) %all-gather.22.cloned.1.call-update) | async-done | bytes 1179664 | tf_op jit(solution)/shard_map/all_gather | solution.py:545
  347.9 55.7 %all-gather.24.cloned.1.call-done.cross_query_ref = bf16[768,768]{1,0:T(8,128)(2,1)} async-done(((bf16[24,768]{1,0:T(8,128)(2,1)}), bf16[768,768]{1,0:T(8,128)(2,1)}) %all-gather.24.cloned.1.call-update) | async-done | bytes 1179664 | tf_op jit(solution)/shard_map/all_gather | solution.py:545
  403.6 55.7 %all-gather.26.cloned.1.call-done.cross_out_ref = bf16[768,768]{1,0:T(8,128)(2,1)} async-done(((bf16[24,768]{1,0:T(8,128)(2,1)}), bf16[768,768]{1,0:T(8,128)(2,1)}) %all-gather.26.cloned.1.call-update) | async-done | bytes 1179664 | tf_op jit(solution)/shard_map/all_gather | solution.py:545
  459.4 65.4 %all-gather.28.cloned.1.call-done.up_ref = bf16[3072,768]{1,0:T(8,128)(2,1)} async-done(((bf16[96,768]{1,0:T(8,128)(2,1)}), bf16[3072,768]{1,0:T(8,128)(2,1)}) %all-gather.28.cloned.1.call-update) | async-done | bytes 4718608 | tf_op jit(solution)/shard_map/all_gather | solution.py:545
  524.8 64.7 %all-gather.30.cloned.1.call-done.down_ref = bf16[768,3072]{1,0:T(8,128)(2,1)} async-done(((bf16[24,3072]{1,0:T(8,128)(2,1)}), bf16[768,3072]{1,0:T(8,128)(2,1)}) %all-gather.30.cloned.1.call-update) | async-done | bytes 4718608 | tf_op jit(solution)/shard_map/all_gather | solution.py:545
  589.5 104.1 %forward.1 = (f32[960,768]{1,0:T(8,128)}, bf16[960,2304]{1,0:T(8,128)(2,1)}, bf16[12,6,160,80]{3,2,1,0:T(8,128)(2,1)}, bf16[960,768]{1,0:T(8,128)(2,1)}, f32[960...) custom-call(s32[24]{0:T(128)} %image_ref.3, ...), custom_call_target="tpu_custom_call" | custom-call | tf_op jit(solution)/shard_map/forward/pallas_call | solution.py:311
  693.6 86.8 %backward.1 = (f32[960,768]{1,0:T(8,128)}, bf16[960,768]{1,0:T(8,128)(2,1)}, bf16[960,768]{1,0:T(8,128)(2,1)}, bf16[960,768]{1,0:T(8,128)(2,1)}, bf16[960,2304]{...) custom-call(s32[24]{0:T(128)} %image_ref.3, ...), custom_call_target="tpu_custom_call" | custom-call | tf_op jit(solution)/shard_map/backward/pallas_call | solution.py:478
  780.4 4.4 convolution_convert_fusion.2
  784.9 3.9 convolution_convert_fusion.3
  788.9 4.0 convolution_convert_fusion.4
  793.0 3.8 convolution_convert_fusion.5
  797.0 3.9 convolution_convert_fusion.6
  800.9 4.5 convolution_convert_fusion.7
  805.5 6.7 bitcast_convert_fusion.1
  812.5 7.7 bitcast_convert_fusion
  820.3 1.3 copy-done.5
  821.6 9.6 convolution_convert_fusion.1
  831.3 1.3 copy-done.4
  832.6 9.4 convolution_convert_fusion
  842.1 10.8 patch_grads.1
  852.9 39.3 %all-reduce.1 = f32[6,768]{1,0:T(8,128)S(1)} all-reduce(f32[6,768]{1,0:T(8,128)S(1)} %slice_add_fusion), channel_id=12, replica_groups=mesh['dp'=32] {'dp'}, use_global_device_ids=true, to_apply=%region_10.0.clone | all-reduce | flops 4608 | bytes 36864
  892.9 1.4 convert_bitcast_fusion.4
  894.3 87.2 %reduce-scatter.20.cloned.1.call-done = bf16[24,768]{1,0:T(8,128)(2,1)} async-done(((bf16[768,768]{1,0:T(8,128)(2,1)}), bf16[24,768]{1,0:T(8,128)(2,1)}) %reduce-scatter.20.cloned.1.call-update) | async-done | bytes 36880 | tf_op jit(solution)/shard_map/reduce_scatter | solution.py:616
  981.5 1.4 convert_bitcast_fusion.5
  982.9 99.8 %reduce-scatter.18.cloned.1.call-done = bf16[24,768]{1,0:T(8,128)(2,1)} async-done(((bf16[768,768]{1,0:T(8,128)(2,1)}), bf16[24,768]{1,0:T(8,128)(2,1)}) %reduce-scatter.18.cloned.1.call-update) | async-done | bytes 36880 | tf_op jit(solution)/shard_map/reduce_scatter | solution.py:616
  1082.7 1.4 convert_bitcast_fusion.6
  1084.1 99.7 %reduce-scatter.16.cloned.1.call-done = bf16[24,768]{1,0:T(8,128)(2,1)} async-done(((bf16[768,768]{1,0:T(8,128)(2,1)}), bf16[24,768]{1,0:T(8,128)(2,1)}) %reduce-scatter.16.cloned.1.call-update) | async-done | bytes 36880 | tf_op jit(solution)/shard_map/reduce_scatter | solution.py:616
  1183.8 1.4 convert_bitcast_fusion.7
  1185.2 99.6 %reduce-scatter.14.cloned.1.call-done = bf16[24,768]{1,0:T(8,128)(2,1)} async-done(((bf16[768,768]{1,0:T(8,128)(2,1)}), bf16[24,768]{1,0:T(8,128)(2,1)}) %reduce-scatter.14.cloned.1.call-update) | async-done | bytes 36880 | tf_op jit(solution)/shard_map/reduce_scatter | solution.py:616
  1284.9 1.4 convert_bitcast_fusion.8
  1286.3 99.6 %reduce-scatter.12.cloned.1.call-done = bf16[24,768]{1,0:T(8,128)(2,1)} async-done(((bf16[768,768]{1,0:T(8,128)(2,1)}), bf16[24,768]{1,0:T(8,128)(2,1)}) %reduce-scatter.12.cloned.1.call-update) | async-done | bytes 36880 | tf_op jit(solution)/shard_map/reduce_scatter | solution.py:616
  1385.9 1.4 convert_bitcast_fusion.9
  1387.3 100.6 %reduce-scatter.22.cloned.1.call-done = bf16[24,1024]{1,0:T(8,128)(2,1)} async-done(((bf16[768,1024]{1,0:T(8,128)(2,1)}), bf16[24,1024]{1,0:T(8,128)(2,1)}) %reduce-scatter.22.cloned.1.call-update) | async-done | bytes 49168 | tf_op jit(solution)/shard_map/reduce_scatter | solution.py:616
  1487.9 1.4 convert_bitcast_fusion.3
  1489.3 100.5 %reduce-scatter.24.cloned.1.call-done = bf16[24,1024]{1,0:T(8,128)(2,1)} async-done(((bf16[768,1024]{1,0:T(8,128)(2,1)}), bf16[24,1024]{1,0:T(8,128)(2,1)}) %reduce-scatter.24.cloned.1.call-update) | async-done | bytes 49168 | tf_op jit(solution)/shard_map/reduce_scatter | solution.py:616
  1589.9 1.4 convert_bitcast_fusion.2
  1591.3 110.7 %reduce-scatter.28.cloned.1.call-done = bf16[96,768]{1,0:T(8,128)(2,1)} async-done(((bf16[3072,768]{1,0:T(8,128)(2,1)}), bf16[96,768]{1,0:T(8,128)(2,1)}) %reduce-scatter.28.cloned.1.call-update) | async-done | bytes 147472 | tf_op jit(solution)/shard_map/reduce_scatter | solution.py:616
  1702.0 1.6 convert_bitcast_fusion.1
  1703.6 110.1 %reduce-scatter.30.cloned.1.call-done = bf16[24,3072]{1,0:T(8,128)(2,1)} async-done(((bf16[768,3072]{1,0:T(8,128)(2,1)}), bf16[24,3072]{1,0:T(8,128)(2,1)}) %reduce-scatter.30.cloned.1.call-update) | async-done | bytes 147472 | tf_op jit(solution)/shard_map/reduce_scatter | solution.py:616
  1813.7 1.6 convert_bitcast_fusion
  (63 shorter events, 10.4 us)
Async XLA Ops:
  7.2 61.3 %all-gather.12.cloned.1.call-start = ((), (), s32[]{:S(2)}) async-start(), calls=%async_computation.10 | async-start | bytes 1622016 | tf_op jit(solution)/shard_map/all_gather | solution.py:545
  7.9 117.3 %all-gather.14.cloned.1.call-start = ((), (), s32[]{:S(2)}) async-start(), calls=%async_computation.11 | async-start | bytes 1622016 | tf_op jit(solution)/shard_map/all_gather | solution.py:545
  8.7 172.4 %all-gather.16.cloned.1.call-start = ((), (), s32[]{:S(2)}) async-start(), calls=%async_computation.12 | async-start | bytes 1216512 | tf_op jit(solution)/shard_map/all_gather | solution.py:545
  9.4 227.3 %all-gather.18.cloned.1.call-start = ((), (), s32[]{:S(2)}) async-start(), calls=%async_computation.13 | async-start | bytes 1216512 | tf_op jit(solution)/shard_map/all_gather | solution.py:545
  10.0 282.3 %all-gather.20.cloned.1.call-start = ((), (), s32[]{:S(2)}) async-start(), calls=%async_computation.14 | async-start | bytes 1216512 | tf_op jit(solution)/shard_map/all_gather | solution.py:545
  10.6 337.3 %all-gather.22.cloned.1.call-start = ((), (), s32[]{:S(2)}) async-start(), calls=%async_computation.15 | async-start | bytes 1216512 | tf_op jit(solution)/shard_map/all_gather | solution.py:545
  11.1 392.5 %all-gather.24.cloned.1.call-start = ((), (), s32[]{:S(2)}) async-start(), calls=%async_computation.16 | async-start | bytes 1216512 | tf_op jit(solution)/shard_map/all_gather | solution.py:545
  11.9 447.5 %all-gather.26.cloned.1.call-start = ((), (), s32[]{:S(2)}) async-start(), calls=%async_computation.17 | async-start | bytes 1216512 | tf_op jit(solution)/shard_map/all_gather | solution.py:545
  12.6 512.2 %all-gather.28.cloned.1.call-start = ((), (), s32[]{:S(2)}) async-start(), calls=%async_computation.18 | async-start | bytes 4866048 | tf_op jit(solution)/shard_map/all_gather | solution.py:545
  13.4 576.2 %all-gather.30.cloned.1.call-start = ((), (), s32[]{:S(2)}) async-start(), calls=%async_computation.19 | async-start | bytes 4866048 | tf_op jit(solution)/shard_map/all_gather | solution.py:545
  14.0 878.9 %reduce-scatter.26.cloned.1.call-start = ((), (), s32[]{:S(2)}) async-start(), calls=%async_computation.27 | async-start | bytes 1216512 | tf_op jit(solution)/shard_map/reduce_scatter | solution.py:616
  780.4 4.5 copy-start.7
  784.8 196.7 %reduce-scatter.20.cloned.1.call-start = ((), (), s32[]{:S(2)}) async-start(), calls=%async_computation.24 | async-start | bytes 1216512 | tf_op jit(solution)/shard_map/reduce_scatter | solution.py:616
  784.9 4.0 copy-start.6
  788.9 293.8 %reduce-scatter.18.cloned.1.call-start = ((), (), s32[]{:S(2)}) async-start(), calls=%async_computation.23 | async-start | bytes 1216512 | tf_op jit(solution)/shard_map/reduce_scatter | solution.py:616
  788.9 4.1 copy-start.1
  793.0 390.8 %reduce-scatter.16.cloned.1.call-start = ((), (), s32[]{:S(2)}) async-start(), calls=%async_computation.22 | async-start | bytes 1216512 | tf_op jit(solution)/shard_map/reduce_scatter | solution.py:616
  796.9 488.0 %reduce-scatter.14.cloned.1.call-start = ((), (), s32[]{:S(2)}) async-start(), calls=%async_computation.21 | async-start | bytes 1216512 | tf_op jit(solution)/shard_map/reduce_scatter | solution.py:616
  800.8 4.7 copy-start
  800.8 585.1 %reduce-scatter.12.cloned.1.call-start = ((), (), s32[]{:S(2)}) async-start(), calls=%async_computation.20 | async-start | bytes 1216512 | tf_op jit(solution)/shard_map/reduce_scatter | solution.py:616
  805.4 682.4 %reduce-scatter.22.cloned.1.call-start = ((), (), s32[]{:S(2)}) async-start(), calls=%async_computation.25 | async-start | bytes 1622016 | tf_op jit(solution)/shard_map/reduce_scatter | solution.py:616
  812.2 777.6 %reduce-scatter.24.cloned.1.call-start = ((), (), s32[]{:S(2)}) async-start(), calls=%async_computation.26 | async-start | bytes 1622016 | tf_op jit(solution)/shard_map/reduce_scatter | solution.py:616
  820.2 1.4 copy-start.5
  820.3 881.7 %reduce-scatter.28.cloned.1.call-start = ((), (), s32[]{:S(2)}) async-start(), calls=%async_computation.28 | async-start | bytes 4866048 | tf_op jit(solution)/shard_map/reduce_scatter | solution.py:616
  831.2 1.4 copy-start.4
  831.2 982.4 %reduce-scatter.30.cloned.1.call-start = ((), (), s32[]{:S(2)}) async-start(), calls=%async_computation.29 | async-start | bytes 4866048 | tf_op jit(solution)/shard_map/reduce_scatter | solution.py:616
  842.0 10.8 copy-start.2
  842.0 10.8 copy-start.3
Sparse Core Ops, SparseCore 0:
  10.8 57.6 all-gather.11
  71.4 53.8 all-gather.13
  128.1 52.9 all-gather.15
  183.8 52.8 all-gather.17
  239.4 52.8 all-gather.19
  295.0 52.8 all-gather.21
  350.8 52.8 all-gather.23
  406.5 52.8 all-gather.25
  462.3 62.4 all-gather.27
  527.6 61.9 all-gather.29
  785.0 95.3 reduce-scatter.25
  885.3 96.1 reduce-scatter.19
  986.6 96.0 reduce-scatter.17
  1087.6 96.1 reduce-scatter.15
  1188.7 96.0 reduce-scatter.13
  1289.8 96.0 reduce-scatter.11
  1391.0 96.8 reduce-scatter.21
  1493.0 96.8 reduce-scatter.23
  1595.3 106.5 reduce-scatter.27
  1707.3 106.3 reduce-scatter.29

commit v2 on v1

--- a/solution.py
+++ b/solution.py
@@ -1,4 +1,6 @@
 import functools
+import itertools
+import math
 
 import jax
 import jax.numpy as jnp
@@ -18,6 +20,8 @@
 VMEM_BYTES = 66_000_000
 MASKED = -1e30
 EPSILON = 1e-06
+TILE_ROWS = 8
+MESH = pl.DeviceIdType.MESH
 F32 = jnp.float32
 BF16 = jnp.bfloat16
 
@@ -541,16 +545,352 @@
 )
 
 
-def gather(shards, norm):
-    full = {name: lax.all_gather(shards[name], "dp", axis=0, tiled=True) for name in NAMES}
-    return full, lax.all_gather(norm, "dp", axis=1, tiled=True)
-
-
-def local(text, patches, segment_ids, row_image, *rest):
+def grid_of(devices):
+    chips = devices // 2
+    outer = math.gcd(chips, 4)
+    rest = chips // outer
+    middle = max(size for size in range(1, math.isqrt(rest) + 1) if rest % size == 0)
+    return outer, middle, rest // middle, 2
+
+
+def device_at(sizes, place):
+    index = 0
+    for size, at in zip(sizes, place):
+        index = index * size + at
+    return index
+
+
+def unflatten(index, sizes):
+    place = []
+    for size in reversed(sizes):
+        place.append(lax.rem(index, size))
+        index = lax.div(index, size)
+    return tuple(reversed(place))
+
+
+def shifted(sizes, place, dim, by):
+    there = [lax.rem(at + by, size) if axis == dim else at for axis, (size, at) in enumerate(zip(sizes, place))]
+    return device_at(sizes, there)
+
+
+def greet(sizes, place):
+    barrier = pltpu.get_barrier_semaphore()
+    count = 0
+    for dim, size in enumerate(sizes):
+        for by in range(1, size):
+            pl.semaphore_signal(barrier, inc=1, device_id=(shifted(sizes, place, dim, by),), device_id_type=MESH)
+            count += 1
+    pl.semaphore_wait(barrier, count)
+
+
+def staged(number, phases):
+    return [
+        (message, stage - message)
+        for stage in range(number + phases)
+        for message in reversed(range(number))
+        if 0 <= stage - message < phases
+    ]
+
+
+ORDERS = ((0, 1, 2, 3), (0, 2, 1, 3))
+
+
+def gather_kernel(sizes, orders, *refs):
+    number = len(orders)
+    shards, fulls = refs[:number], refs[number : 2 * number]
+    send_sem, recv_sem, own_sem = refs[2 * number :]
+    place = unflatten(lax.axis_index("dp"), sizes)
+    greet(sizes, place)
+    me = device_at(sizes, place)
+    last = len(sizes)
+    zero = (0,) * last
+    sends = []
+
+    def block(message, owner):
+        rows = shards[message].shape[1]
+        return fulls[message].at[:, pl.ds(owner * rows, rows), :]
+
+    def owner_of(offset):
+        return device_at(sizes, [lax.rem(at + size - back, size) for at, size, back in zip(place, sizes, offset)])
+
+    def forward(message, offset, phase):
+        owner = owner_of(offset)
+        source = block(message, owner) if any(offset) else shards[message]
+        for dim in orders[message][phase:]:
+            for by in range(1, sizes[dim]):
+                slot = device_at(sizes, [at + by if axis == dim else at for axis, at in enumerate(offset)])
+                copy = pltpu.make_async_remote_copy(
+                    src_ref=source,
+                    dst_ref=block(message, owner),
+                    send_sem=send_sem.at[message, slot],
+                    recv_sem=recv_sem.at[message, slot],
+                    device_id=(shifted(sizes, place, dim, by),),
+                    device_id_type=MESH,
+                )
+                copy.start()
+                sends.append(copy)
+
+    def arrivals(message, phase):
+        order = orders[message]
+        free = [
+            range(size)
+            if dim in order[: phase - 1]
+            else (range(1, size) if dim == order[phase - 1] else range(1))
+            for dim, size in enumerate(sizes)
+        ]
+        return itertools.product(*free)
+
+    def arrived(message, offset):
+        there = block(message, owner_of(offset))
+        pltpu.make_async_copy(there, there, recv_sem.at[message, device_at(sizes, offset)]).wait()
+
+    held = [pltpu.make_async_copy(shards[at], block(at, me), own_sem.at[at]) for at in range(number)]
+    for copy in held:
+        copy.start()
+    for message in range(number):
+        forward(message, zero, 0)
+    for message, phase in staged(number, last):
+        if phase > 0:
+            for offset in arrivals(message, phase):
+                arrived(message, offset)
+                forward(message, offset, phase)
+    for message in range(number):
+        for offset in arrivals(message, last):
+            arrived(message, offset)
+    for copy in held:
+        copy.wait()
+    for copy in sends:
+        copy.wait_send()
+
+
+def gather_all(shards, orders, devices):
+    number = len(shards)
+    return pl.pallas_call(
+        functools.partial(gather_kernel, grid_of(devices), orders),
+        in_specs=[pl.BlockSpec(memory_space=pltpu.VMEM)] * number,
+        out_specs=[pl.BlockSpec(memory_space=pl.ANY)] * number,
+        out_shape=[
+            jax.ShapeDtypeStruct((shard.shape[0], shard.shape[1] * devices, shard.shape[2]), shard.dtype)
+            for shard in shards
+        ],
+        scratch_shapes=[
+            pltpu.SemaphoreType.DMA((number, devices)),
+            pltpu.SemaphoreType.DMA((number, devices)),
+            pltpu.SemaphoreType.DMA((number,)),
+        ],
+        compiler_params=pltpu.CompilerParams(collective_id=0, has_side_effects=True),
+        name="gather_all",
+    )(*shards)
+
+
+def scatter_kernel(sizes, orders, *refs):
+    number = len(orders)
+    grads, outs = refs[:number], refs[number : 2 * number]
+    own, core, firsts, seconds, lasts = [
+        refs[number * (2 + at) : number * (3 + at)] for at in range(5)
+    ]
+    load_sem, send_sem, recv_sem = refs[7 * number :]
+    place = unflatten(lax.axis_index("dp"), sizes)
+    side = place[3]
+    greet(sizes, place)
+    sends = []
+
+    def remote(message, source, target, dim, by, slot):
+        copy = pltpu.make_async_remote_copy(
+            src_ref=source,
+            dst_ref=target,
+            send_sem=send_sem.at[message, slot],
+            recv_sem=recv_sem.at[message, slot],
+            device_id=(shifted(sizes, place, dim, by),),
+            device_id_type=MESH,
+        )
+        copy.start()
+        sends.append(copy)
+
+    def got(message, target, slot):
+        pltpu.make_async_copy(target, target, recv_sem.at[message, slot]).wait()
+
+    def slot_of(dim, by):
+        return sum(sizes[:dim]) - dim + by
+
+    def send(message, held, dims, dim, target):
+        for by in range(1, sizes[dim]):
+            there = lax.rem(place[dim] + by, sizes[dim])
+            at = tuple(there if axis == dim else slice(None) for axis in dims)
+            remote(message, held.at[at], target.at[by - 1], dim, by, slot_of(dim, by))
+
+    def reduce(message, held, dims, dim, target, store):
+        rest = [axis for axis in dims if axis != dim]
+        for by in range(1, sizes[dim]):
+            got(message, target.at[by - 1], slot_of(dim, by))
+
+        def body(index, carry):
+            at = unflatten(index, [sizes[axis] for axis in rest])
+            full = list(at)
+            full.insert(dims.index(dim), place[dim])
+            total = held[tuple(full)].astype(F32)
+            for by in range(1, sizes[dim]):
+                total += target[(by - 1, *at)].astype(F32)
+            store(at, total)
+            return carry
+
+        lax.fori_loop(0, math.prod(sizes[axis] for axis in rest), body, 0)
+        return rest
+
+    loads = []
+    for message in range(number):
+        remote(message, grads[message].at[:, :, :, 1 - side], core[message], 3, 1, 0)
+        load = pltpu.make_async_copy(grads[message].at[:, :, :, side], own[message], load_sem.at[message])
+        load.start()
+        loads.append(load)
+
+    def keep(ref, lead):
+        def store(at, total):
+            ref[(*lead, *at)] = total.astype(ref.dtype)
+
+        return store
+
+    def store_out(message):
+        def store(at, total):
+            outs[message][...] = total
+
+        return store
+
+    def step(message, phase):
+        last, middle, first = orders[message][:3]
+        everything = [0, 1, 2]
+        if phase == 0:
+            loads[message].wait()
+            got(message, core[message], 0)
+
+            def body(index, carry):
+                at = unflatten(index, sizes[:3])
+                total = own[message][at].astype(F32) + core[message][at].astype(F32)
+                own[message][at] = total.astype(own[message].dtype)
+                return carry
+
+            lax.fori_loop(0, math.prod(sizes[:3]), body, 0)
+            send(message, own[message], everything, first, firsts[message])
+        elif phase == 1:
+            rest = reduce(message, own[message], everything, first, firsts[message], keep(firsts[message], (0,)))
+            send(message, firsts[message].at[0], rest, middle, seconds[message])
+        elif phase == 2:
+            rest = [axis for axis in everything if axis != first]
+            rest = reduce(message, firsts[message].at[0], rest, middle, seconds[message], keep(seconds[message], (0,)))
+            send(message, seconds[message].at[0], rest, last, lasts[message])
+        else:
+            reduce(message, seconds[message].at[0], [last], last, lasts[message], store_out(message))
+
+    for message in range(number):
+        step(message, 0)
+    for message, phase in staged(number, 4):
+        if phase > 0:
+            step(message, phase)
+    for copy in sends:
+        copy.wait_send()
+
+
+def scatter_all(grads, orders, devices):
+    sizes = grid_of(devices)
+    number = len(grads)
+    split = [grad.reshape(*sizes, grad.shape[0] // devices, *grad.shape[1:]) for grad in grads]
+    blocks = [(array.shape[4:], array.dtype) for array in split]
+
+    def scratch(drop, lead):
+        made = []
+        for (shape, dtype), order in zip(blocks, orders):
+            gone = order[3 - drop : 3]
+            outer = [sizes[gone[0]] - 1] if lead else []
+            made.append(pltpu.VMEM((*outer, *[sizes[axis] for axis in range(3) if axis not in gone], *shape), dtype))
+        return made
+
+    slots = sum(sizes) - 3
+    return pl.pallas_call(
+        functools.partial(scatter_kernel, sizes, orders),
+        in_specs=[pl.BlockSpec(memory_space=pl.ANY)] * number,
+        out_specs=[pl.BlockSpec(memory_space=pltpu.VMEM)] * number,
+        out_shape=[jax.ShapeDtypeStruct(shape, F32) for shape, _ in blocks],
+        scratch_shapes=[
+            *scratch(0, False),
+            *scratch(0, False),
+            *scratch(1, True),
+            *scratch(2, True),
+            *scratch(3, True),
+            pltpu.SemaphoreType.DMA((number,)),
+            pltpu.SemaphoreType.DMA((number, slots)),
+            pltpu.SemaphoreType.DMA((number, slots)),
+        ],
+        compiler_params=pltpu.CompilerParams(collective_id=1, has_side_effects=True, vmem_limit_bytes=VMEM_BYTES),
+        name="scatter_all",
+    )(*split)
+
+
+GATHER_ORDERS = {
+    "query": 1,
+    "key": 0,
+    "value": 1,
+    "out": 0,
+    "cross_key": 1,
+    "cross_value": 0,
+    "cross_query": 1,
+    "cross_out": 0,
+    "up": 1,
+    "down": 0,
+}
+
+
+def aligned(devices, shards):
+    return devices > 2 and devices % 2 == 0 and all(shard.shape[0] % TILE_ROWS == 0 for shard in shards.values())
+
+
+def gather(devices, shards, norm):
+    if not aligned(devices, shards):
+        full = {name: lax.all_gather(shards[name], "dp", axis=0, tiled=True) for name in NAMES}
+        return full, lax.all_gather(norm, "dp", axis=1, tiled=True)
+    rows, width = norm.shape
+    padded = jnp.zeros((1, TILE_ROWS, LANES), norm.dtype).at[0, :rows, :width].set(norm)
+    blocks = [padded] + [shards[name][None] for name in GATHER_ORDERS]
+    orders = [ORDERS[0]] + [ORDERS[at] for at in GATHER_ORDERS.values()]
+    norms, *fulls = gather_all(blocks, orders, devices)
+    norms = norms.reshape(devices, TILE_ROWS, LANES)[:, :rows, :width]
+    norms = jnp.swapaxes(norms, 0, 1).reshape(rows, devices * width)
+    return {name: array[0] for name, array in zip(GATHER_ORDERS, fulls)}, norms
+
+
+SCATTER_ORDERS = {
+    "down": 0,
+    "up": 1,
+    "cross_key": 0,
+    "cross_value": 1,
+    "query": 0,
+    "key": 1,
+    "value": 0,
+    "out": 1,
+    "cross_query": 0,
+    "cross_out": 1,
+}
+
+
+def scatter(devices, shards, grads, norm):
+    if not aligned(devices, shards):
+        parts = [lax.psum_scatter(grads[name], "dp", scatter_dimension=0, tiled=True) for name in NAMES]
+        return [part.astype(F32) for part in parts], lax.psum_scatter(norm, "dp", scatter_dimension=1, tiled=True)
+    rows, width = norm.shape
+    width //= devices
+    norm = jnp.swapaxes(norm.reshape(rows, devices, width), 0, 1)
+    padded = jnp.zeros((devices, TILE_ROWS, LANES), F32).at[:, :rows, :width].set(norm)
+    blocks = [grads[name] for name in SCATTER_ORDERS] + [padded.reshape(devices * TILE_ROWS, LANES)]
+    orders = [ORDERS[at] for at in SCATTER_ORDERS.values()] + [ORDERS[0]]
+    *parts, norm = scatter_all(blocks, orders, devices)
+    parts = dict(zip(SCATTER_ORDERS, parts))
+    return [parts[name] for name in NAMES], norm[:rows, :width]
+
+
+def local(devices, text, patches, segment_ids, row_image, *rest):
     *shards, norm_params, cotangent = rest
     shards = {name: jnp.swapaxes(shard, 0, 1) for name, shard in zip(NAMES, shards, strict=True)}
     rows, length, width = text.shape
-    weights, norms = gather(shards, norm_params)
+    weights, norms = gather(devices, shards, norm_params)
     norms = norms.astype(F32)
     norms = jnp.concatenate([norms, jnp.zeros((2, width), F32)], axis=0)
     ids = segment_ids + 8 * jnp.arange(rows, dtype=jnp.int32)[:, None]
@@ -610,18 +950,13 @@
         (grad_pre, second_low),
         (branch_three, hidden),
     )
-    grads = []
-    for left, right in products:
-        grad = tn(left, right).astype(BF16)
-        grads.append(lax.psum_scatter(grad, "dp", scatter_dimension=0, tiled=True))
-    norm_grad = lax.psum_scatter(
-        (norm_late + norm_early)[:6], "dp", scatter_dimension=1, tiled=True
-    )
+    sums = {name: tn(left, right).astype(BF16) for name, (left, right) in zip(NAMES, products, strict=True)}
+    grads, norm_grad = scatter(devices, shards, sums, (norm_late + norm_early)[:6])
     return (
         output.reshape(text.shape),
         text_grad.reshape(text.shape),
         patch_grad,
-        *[jnp.swapaxes(grad, 0, 1).astype(F32) for grad in grads],
+        *[jnp.swapaxes(grad, 0, 1) for grad in grads],
         norm_grad,
     )
 
@@ -631,4 +966,5 @@
     columns = P(None, "dp")
     in_specs = (split, split, P("dp", None), P("dp"), *([columns] * 11), split)
     out_specs = (split, split, split, *([columns] * 11))
-    return jax.shard_map(local, mesh=mesh, in_specs=in_specs, out_specs=out_specs, check_vma=False)
+    program = functools.partial(local, mesh.shape["dp"])
+    return jax.shard_map(program, mesh=mesh, in_specs=in_specs, out_specs=out_specs, check_vma=False)

time: 1830 us -> 523 us (0.29)
  waiting for transfers between devices: 1430 us -> 0 us
  Pallas kernels: 212 us -> 451 us
  blocking collectives: 83.2 us -> 0 us
    reduce_scatter x10 -> x0, waiting for transfers between devices: 908 us -> none  [local(): grads.append(lax.psum_scatter(grad, 'dp', scatter_dimension=0, tiled=True))]
    all_gather x10 -> x0, waiting for transfers between devices: 518 us -> none  [gather(): lax.all_gather(shards[name], 'dp', axis=0, tiled=True)]
    pallas_call x0 -> x2, Pallas kernels: none -> 239 us  [the longest x1 141 us: scatter_all(): pl.pallas_call(functools.partial(scatter_kernel, sizes, orders), in_specs...]
    all_gather x1 -> x0, blocking collectives: 43.9 us -> none  [gather(): return (full, lax.all_gather(norm, 'dp', axis=1, tiled=True))]
    unnamed x1 -> x0, blocking collectives: 39.3 us -> none
  transfers between devices with their start and end apart: 20 -> 0, of which waited for: 19 -> 0; matrix products, arithmetic and copies ran while one was open for 4% -> 0% of each run, Pallas kernels for 1% -> 0%
where the time goes in v2:
time: 523 us; the launch traced here: 518 us
  Pallas kernels  451 us (86%)
  matrix products  44 us (8%)
  local copies, waits for them, and re-layouts  20 us (4%)
    pallas_call x1, Pallas kernels, scatter_all(): pl.pallas_call(functools.partial(scatter_kernel, sizes, orders), in_specs...  141 us
    pallas_call x1, Pallas kernels, forward(): pl.pallas_call(functools.partial(forward_kernel, patch_count), grid_spec=...  104 us
    pallas_call x1, Pallas kernels, gather_all(): pl.pallas_call(functools.partial(gather_kernel, grid_of(devices), orders)...  97.4 us
    pallas_call x1, Pallas kernels, backward(): pl.pallas_call(backward_kernel, grid_spec=pltpu.PrefetchScalarGridSpec(nu...  86.8 us
    dot_general x10, matrix products, tn(): lax.dot_general(left, right, (((0,), (0,)), ((), ())), preferred_element_...  44 us
    unnamed x45, local copies, waits for them, and re-layouts  16.2 us
    pallas_call x1, Pallas kernels, patch_grads(): pl.pallas_call(patch_kernel, grid=(images // IMAGE_BLOCK,), in_specs=[blo...  11 us

profile of v2, /device:TPU:0, one launch (start us, length us, event | category | flops | bytes accessed | tf_op | source)
XLA Modules:
  0.0 518.0 jit_solution(1258734785549238002)
XLA Ops:
  0.7 1.3 scatter.6.refs_0_
  1.9 0.8 broadcast_add_fusion
  2.7 0.7 reshape.169.id_row_ref
  3.4 1.0 reshape.188.id_column_ref
  4.4 97.4 %gather_all.1 = (bf16[1,256,128]{2,1,0:T(8,128)(2,1)}, bf16[1,768,768]{2,1,0:T(8,128)(2,1)}, bf16[1,768,768]{2,1,0:T(8,128)(2,1)}, bf16[1,768,768]{2,1,0:T(8,128...) custom-call(bf16[1,8,128]{2,1,0:T(8,128)(2,1)} %scatter.6.refs_0_, ...), custom_call_target="tpu_custom_call" | custom-call | tf_op jit(solution)/shard_map/gather_all/pallas_call | solution.py:668
  101.7 0.8 copy.38
  102.6 0.1 convert_element_type.38
  102.7 0.6 pad_convert_fusion.norm_ref
  103.3 10.1 %image_rows.1 = (bf16[12,160,1024]{2,1,0:T(8,128)(2,1)}, bf16[12,160,768]{2,1,0:T(8,128)(2,1)}, bf16[12,160,768]{2,1,0:T(8,128)(2,1)}) custom-call(bf16[12,145,1024]{2,1,0:T(8,128)(2,1)} %patches_ref.1, bf16[768,1024]{1,0:T(8,128)(2,1)} %bitcast.94, bf16[768,1024]{1,0:T(8,128)(2,1)} %bitcast.96), custom_call_target="tpu_custom_call" | custom-call | tf_op jit(solution)/shard_map/image_rows/pallas_call | solution.py:98
  113.4 104.2 %forward.1 = (f32[960,768]{1,0:T(8,128)}, bf16[960,2304]{1,0:T(8,128)(2,1)}, bf16[12,6,160,80]{3,2,1,0:T(8,128)(2,1)}, bf16[960,768]{1,0:T(8,128)(2,1)}, f32[960...) custom-call(s32[24]{0:T(128)} %image_ref.3, ...), custom_call_target="tpu_custom_call" | custom-call | tf_op jit(solution)/shard_map/forward/pallas_call | solution.py:315
  217.7 0.0 copy-start.13
  217.7 9.2 %convolution_convert_fusion.1 = bf16[768,3072]{1,0:T(8,128)(2,1)} fusion(bf16[960,768]{1,0:T(8,128)(2,1)} %get-tuple-element.111, bf16[960,3072]{1,0:T(8,128)(2,1)} %get-tuple-element.112), kind=kOutput, calls=%fused_computation.1 | convolution fusion | flops 4532207616 | bytes 12091392 | tf_op jit(solution)/shard_map/dot_general | solution.py:38
  226.9 0.0 copy-done.13
  226.9 6.9 %convolution_convert_fusion = bf16[3072,768]{1,0:T(8,128)(2,1)} fusion(bf16[960,3072]{1,0:T(8,128)(2,1)S(1)} %copy-done.7, bf16[960,768]{1,0:T(8,128)(2,1)S(1)} %copy-done.13), kind=kOutput, calls=%fused_computation | convolution fusion | flops 4532207616 | bytes 12091392 | tf_op jit(solution)/shard_map/dot_general | solution.py:38
  233.8 86.8 %backward.1 = (f32[960,768]{1,0:T(8,128)}, bf16[960,768]{1,0:T(8,128)(2,1)}, bf16[960,768]{1,0:T(8,128)(2,1)}, bf16[960,768]{1,0:T(8,128)(2,1)}, bf16[960,2304]{...) custom-call(s32[24]{0:T(128)} %image_ref.3, ...), custom_call_target="tpu_custom_call" | custom-call | tf_op jit(solution)/shard_map/backward/pallas_call | solution.py:482
  320.6 0.7 slice_add_fusion
  321.3 4.4 convolution_convert_fusion.2
  325.8 0.0 copy-done.10
  325.8 0.0 copy-start.11
  325.8 2.5 convolution_convert_fusion.3
  328.3 2.5 convolution_convert_fusion.4
  330.8 0.1 reshape.185
  330.9 0.0 slice-start
  330.9 0.1 copy.36
  331.0 0.7 scatter.9.clone
  331.6 4.3 convolution_convert_fusion.5
  335.9 0.0 slice-done.1
  335.9 2.5 convolution_convert_fusion.6
  338.4 2.5 convolution_convert_fusion.7
  340.9 0.9 copy-done.8
  341.9 4.6 bitcast_convert_fusion.1
  346.5 4.6 bitcast_convert_fusion
  351.1 11.0 %patch_grads.1 = f32[12,145,1024]{2,1,0:T(8,128)} custom-call(bf16[12,160,768]{2,1,0:T(8,128)(2,1)} %get-tuple-element.109.keys_ref, bf16[12,160,768]{2,1,0:T(8,128)(2,1)} %get-tuple-element.110.values_ref, bf16[768,1024]{1,0:T(8,128)(2,1)} %bitcast.95, bf16[768,1024]{1,0:T(8,128)(2,1)} %bitcast.97), custom_call_target="tpu_custom_call" | custom-call | tf_op jit(solution)/shard_map/patch_grads/pallas_call | solution.py:126
  362.1 141.4 %scatter_all.1 = (f32[24,3072]{1,0:T(8,128)}, f32[96,768]{1,0:T(8,128)}, f32[24,1024]{1,0:T(8,128)}, f32[24,1024]{1,0:T(8,128)}, f32[24,768]{1,0:T(8,128)}, /*in...) custom-call(bf16[4,2,2,2,24,3072]{5,4,3,2,1,0:T(8,128)(2,1)} %bitcas, ...), custom_call_target="tpu_custom_call" | custom-call | tf_op jit(solution)/shard_map/scatter_all/pallas_call | solution.py:808
  503.5 0.0 copy-start.4
  503.5 0.0 copy-start.3
  503.5 0.0 copy-start.6
  503.5 1.6 copy.50
  505.1 1.5 copy.51
  506.6 1.5 copy.52
  508.1 1.5 copy.53
  509.7 1.5 copy.54
  511.2 1.5 copy.55
  512.7 1.5 copy.56
  514.3 1.5 copy.57
  515.8 0.7 copy.58
  516.5 0.7 copy.59
  517.2 0.6 copy.60
  (24 shorter events, 0.0 us)
Async XLA Ops:
  217.7 9.2 %copy-start.7 = (bf16[960,3072]{1,0:T(8,128)(2,1)S(1)}, bf16[960,3072]{1,0:T(8,128)(2,1)}, u32[]{:S(2)}) copy-start(bf16[960,3072]{1,0:T(8,128)(2,1)} %get-tuple-element.113) | copy-start | bytes 17694724
  217.7 9.2 %copy-start.13 = (bf16[960,768]{1,0:T(8,128)(2,1)S(1)}, bf16[960,768]{1,0:T(8,128)(2,1)}, u32[]{:S(2)}) copy-start(bf16[960,768]{1,0:T(8,128)(2,1)} %get-tuple-element.114) | copy-start | bytes 4423684
  233.8 86.8 %copy-start.5 = (f32[8,768]{1,0:T(8,128)S(1)}, f32[8,768]{1,0:T(8,128)}, u32[]{:S(2)}) copy-start(f32[8,768]{1,0:T(8,128)} %get-tuple-element.123) | copy-start | bytes 73732
  321.3 4.4 copy-start.10
  321.3 4.4 copy-start.12
  325.8 2.5 copy-start.9
  325.8 2.5 copy-start.11
  328.3 3.4 copy-start.2
  330.9 5.0 slice-start
  331.6 4.3 slice-start.1
  338.4 2.5 copy-start
  338.4 3.4 copy-start.8
  341.9 4.6 copy-start.1
  503.5 12.3 %copy-start.4 = (f32[96,768]{1,0:T(8,128)S(1)}, f32[96,768]{1,0:T(8,128)}, u32[]{:S(2)}) copy-start(f32[96,768]{1,0:T(8,128)} %get-tuple-element.133) | copy-start | bytes 884740
  503.5 13.0 %copy-start.3 = (f32[24,3072]{1,0:T(8,128)S(1)}, f32[24,3072]{1,0:T(8,128)}, u32[]{:S(2)}) copy-start(f32[24,3072]{1,0:T(8,128)} %get-tuple-element.134) | copy-start | bytes 884740
  503.5 13.7 %copy-start.6 = (f32[8,128]{1,0:T(8,128)S(1)}, f32[8,128]{1,0:T(8,128)}, u32[]{:S(2)}) copy-start(f32[8,128]{1,0:T(8,128)} %get-tuple-element.135) | copy-start | bytes 12292

commit v3 on v2

--- a/solution.py
+++ b/solution.py
@@ -1,6 +1,7 @@
 import functools
 import itertools
 import math
+from typing import NamedTuple
 
 import jax
 import jax.numpy as jnp
@@ -683,15 +684,42 @@
     )(*shards)
 
 
-def scatter_kernel(sizes, orders, *refs):
-    number = len(orders)
-    grads, outs = refs[:number], refs[number : 2 * number]
-    own, core, firsts, seconds, lasts = [
-        refs[number * (2 + at) : number * (3 + at)] for at in range(5)
-    ]
-    load_sem, send_sem, recv_sem = refs[7 * number :]
+LAGS = (1, 3, 5, 7)
+
+
+class Message(NamedTuple):
+    order: tuple
+    rows: int
+    width: int
+    dtype: type
+    out: int
+    at: tuple
+    start: int
+    ring: int
+    slot: int
+
+
+class Job(NamedTuple):
+    left: int
+    left_start: int
+    right: int
+    right_start: int
+    width: int
+    messages: tuple
+    plane: int | None
+
+
+def products_kernel(sizes, jobs, messages, number_in, number_out, number_rings, *refs):
+    count = len(messages)
+    inputs, norm = refs[:number_in], refs[number_in]
+    outs = refs[number_in + 1 : number_in + 1 + number_out]
+    refs = refs[number_in + 1 + number_out :]
+    own, core, firsts, seconds, lasts = [refs[count * at : count * (at + 1)] for at in range(5)]
+    rings = refs[5 * count : 5 * count + number_rings]
+    lefts, rights, product, job_sem, load_sem, send_sem, recv_sem = refs[5 * count + number_rings :]
     place = unflatten(lax.axis_index("dp"), sizes)
     side = place[3]
+    blocks = math.prod(sizes[:3])
     greet(sizes, place)
     sends = []
 
@@ -705,7 +733,7 @@
             device_id_type=MESH,
         )
         copy.start()
-        sends.append(copy)
+        return copy
 
     def got(message, target, slot):
         pltpu.make_async_copy(target, target, recv_sem.at[message, slot]).wait()
@@ -717,7 +745,7 @@
         for by in range(1, sizes[dim]):
             there = lax.rem(place[dim] + by, sizes[dim])
             at = tuple(there if axis == dim else slice(None) for axis in dims)
-            remote(message, held.at[at], target.at[by - 1], dim, by, slot_of(dim, by))
+            sends.append(remote(message, held.at[at], target.at[by - 1], dim, by, slot_of(dim, by)))
 
     def reduce(message, held, dims, dim, target, store):
         rest = [axis for axis in dims if axis != dim]
@@ -737,92 +765,201 @@
         lax.fori_loop(0, math.prod(sizes[axis] for axis in rest), body, 0)
         return rest
 
-    loads = []
-    for message in range(number):
-        remote(message, grads[message].at[:, :, :, 1 - side], core[message], 3, 1, 0)
-        load = pltpu.make_async_copy(grads[message].at[:, :, :, side], own[message], load_sem.at[message])
-        load.start()
-        loads.append(load)
-
-    def keep(ref, lead):
+    def keep(ref):
         def store(at, total):
-            ref[(*lead, *at)] = total.astype(ref.dtype)
+            ref[(0, *at)] = total.astype(ref.dtype)
 
         return store
 
     def store_out(message):
         def store(at, total):
-            outs[message][...] = total
+            columns = slice(message.start, message.start + message.width)
+            outs[message.out][(*message.at, slice(None), columns)] = total
 
         return store
 
-    def step(message, phase):
-        last, middle, first = orders[message][:3]
+    loads = {}
+    exchanges = {}
+
+    def step(index, phase):
+        message = messages[index]
+        last, middle, first = message.order[:3]
         everything = [0, 1, 2]
         if phase == 0:
-            loads[message].wait()
-            got(message, core[message], 0)
-
-            def body(index, carry):
-                at = unflatten(index, sizes[:3])
-                total = own[message][at].astype(F32) + core[message][at].astype(F32)
-                own[message][at] = total.astype(own[message].dtype)
+            if index in loads:
+                loads[index].wait()
+            got(index, core[index], 0)
+
+            def body(step, carry):
+                at = unflatten(step, sizes[:3])
+                total = own[index][at].astype(F32) + core[index][at].astype(F32)
+                own[index][at] = total.astype(own[index].dtype)
                 return carry
 
-            lax.fori_loop(0, math.prod(sizes[:3]), body, 0)
-            send(message, own[message], everything, first, firsts[message])
+            lax.fori_loop(0, blocks, body, 0)
+            send(index, own[index], everything, first, firsts[index])
         elif phase == 1:
-            rest = reduce(message, own[message], everything, first, firsts[message], keep(firsts[message], (0,)))
-            send(message, firsts[message].at[0], rest, middle, seconds[message])
+            rest = reduce(index, own[index], everything, first, firsts[index], keep(firsts[index]))
+            send(index, firsts[index].at[0], rest, middle, seconds[index])
         elif phase == 2:
             rest = [axis for axis in everything if axis != first]
-            rest = reduce(message, firsts[message].at[0], rest, middle, seconds[message], keep(seconds[message], (0,)))
-            send(message, seconds[message].at[0], rest, last, lasts[message])
+            rest = reduce(index, firsts[index].at[0], rest, middle, seconds[index], keep(seconds[index]))
+            send(index, seconds[index].at[0], rest, last, lasts[index])
         else:
-            reduce(message, seconds[message].at[0], [last], last, lasts[message], store_out(message))
-
-    for message in range(number):
-        step(message, 0)
-    for message, phase in staged(number, 4):
-        if phase > 0:
-            step(message, phase)
+            reduce(index, seconds[index].at[0], [last], last, lasts[index], store_out(message))
+
+    tail = count - 1
+    exchanges[tail] = remote(tail, norm.at[:, :, :, 1 - side], core[tail], 3, 1, 0)
+    loads[tail] = pltpu.make_async_copy(norm.at[:, :, :, side], own[tail], load_sem)
+    loads[tail].start()
+
+    def load(at):
+        job = jobs[at]
+        pair = []
+        for which, (index, start, width, slots) in enumerate(
+            ((job.left, job.left_start, lefts.shape[2], lefts), (job.right, job.right_start, job.width, rights))
+        ):
+            source = inputs[index]
+            target = slots.at[at % 2, pl.ds(0, source.shape[0]), pl.ds(0, width)]
+            pair.append(pltpu.make_async_copy(source.at[:, pl.ds(start, width)], target, job_sem.at[at, which]))
+            pair[-1].start()
+        return pair
+
+    holder = {}
+
+    def produce(at):
+        job = jobs[at]
+        depth = inputs[job.left].shape[0]
+        half = lefts.shape[2] // 2
+
+        def multiply(part, carry):
+            lanes = pl.ds(pl.multiple_of(part * half, half), half)
+            product[lanes, : job.width] = tn(lefts[at % 2, :depth, lanes], rights[at % 2, :depth, : job.width])
+            return carry
+
+        lax.fori_loop(0, 2, multiply, 0)
+        for part, index in enumerate(job.messages):
+            message = messages[index]
+            if holder.get((message.ring, message.slot), index) != index:
+                exchanges.pop(holder[message.ring, message.slot]).wait_send()
+            holder[message.ring, message.slot] = index
+            columns = slice(part * message.width, (part + 1) * message.width)
+            steps = blocks if job.plane is None else blocks // sizes[0]
+
+            def split(step, carry):
+                where = unflatten(step, sizes[:3] if job.plane is None else sizes[1:3])
+                where = where if job.plane is None else (job.plane, *where)
+                base = pl.multiple_of(step * 2 * message.rows, TILE_ROWS)
+                even = product[pl.ds(base, message.rows), columns]
+                odd = product[pl.ds(base + message.rows, message.rows), columns]
+                own[index][where] = jnp.where(side == 0, even, odd).astype(BF16)
+                rings[message.ring][(message.slot, *where)] = jnp.where(side == 0, odd, even).astype(BF16)
+                return carry
+
+            lax.fori_loop(0, steps, split, 0)
+            if job.plane in (None, sizes[0] - 1):
+                exchanges[index] = remote(index, rings[message.ring].at[message.slot], core[index], 3, 1, 0)
+
+    made = {tail: 0}
+    pending = load(0)
+    end = max(LAGS) + len(jobs)
+    for tick in range(end + 1):
+        if tick < len(jobs):
+            following = load(tick + 1) if tick + 1 < len(jobs) else None
+            for copy in pending:
+                copy.wait()
+            produce(tick)
+            pending = following
+            if jobs[tick].plane in (None, sizes[0] - 1):
+                made.update({index: tick for index in jobs[tick].messages})
+        for phase, lag in enumerate(LAGS):
+            for index in sorted(made):
+                if made[index] + lag == tick:
+                    step(index, phase)
     for copy in sends:
         copy.wait_send()
-
-
-def scatter_all(grads, orders, devices):
+    for copy in exchanges.values():
+        copy.wait_send()
+
+
+def weight_grads(devices, inputs, norm):
     sizes = grid_of(devices)
-    number = len(grads)
-    split = [grad.reshape(*sizes, grad.shape[0] // devices, *grad.shape[1:]) for grad in grads]
-    blocks = [(array.shape[4:], array.dtype) for array in split]
+    names = list(inputs)
+    at = {name: index for index, name in enumerate(names)}
+    width = inputs["tokens"].shape[1]
+    rows = width // devices
+    patch_width = inputs["padded"].shape[1]
+    hidden = inputs["hidden"].shape[1]
+    planes = hidden // width
+    third = width // 3
+    outs = [(6, rows, width), (2, rows, patch_width), (planes * rows, width), (rows, hidden), (TILE_ROWS, LANES)]
+    rings = [(2, rows, patch_width), (3, planes * rows, third), (2, rows, width)]
+    jobs, messages = [], []
+
+    def message(which, *rest):
+        messages.append(Message(ORDERS[which], *rest))
+        return len(messages) - 1
+
+    for part in range(hidden // patch_width):
+        start = part * patch_width
+        index = message(part % 2, rows, patch_width, BF16, 3, (), start, 0, part % 2)
+        jobs.append(Job(at["branch_three"], 0, at["hidden"], start, patch_width, (index,), None))
+    ups = tuple(
+        message((part + 1) % 2, planes * rows, third, BF16, 2, (), part * third, 1, part) for part in range(3)
+    )
+    for plane in range(sizes[0]):
+        jobs.append(Job(at["grad_pre"], plane * width, at["second_low"], 0, width, ups, plane))
+    for part, left in enumerate(("grad_keys", "grad_values")):
+        index = message(part, rows, patch_width, BF16, 1, (part,), 0, 0, (part + 1) % 2)
+        jobs.append(Job(at[left], 0, at["padded"], 0, patch_width, (index,), None))
+    pairs = (
+        ("branch_two", 0, "mixed_cross", 5),
+        ("grad_cross", 0, "first_low", 4),
+        ("branch_one", 0, "mixed_self", 3),
+        ("grad_qkv", 0, "tokens", 0),
+        ("grad_qkv", width, "tokens", 1),
+        ("grad_qkv", 2 * width, "tokens", 2),
+    )
+    for part, (left, start, right, out) in enumerate(pairs):
+        index = message(part % 2, rows, width, BF16, 0, (out,), 0, 2, part % 2)
+        jobs.append(Job(at[left], start, at[right], 0, width, (index,), None))
+    message(0, TILE_ROWS, LANES, F32, 4, (), 0, 0, 0)
+    count = len(messages)
 
     def scratch(drop, lead):
         made = []
-        for (shape, dtype), order in zip(blocks, orders):
-            gone = order[3 - drop : 3]
+        for item in messages:
+            gone = item.order[3 - drop : 3]
             outer = [sizes[gone[0]] - 1] if lead else []
-            made.append(pltpu.VMEM((*outer, *[sizes[axis] for axis in range(3) if axis not in gone], *shape), dtype))
+            shape = (*outer, *[sizes[axis] for axis in range(3) if axis not in gone], item.rows, item.width)
+            made.append(pltpu.VMEM(shape, item.dtype))
         return made
 
     slots = sum(sizes) - 3
+    deep = max(array.shape[0] for array in inputs.values())
     return pl.pallas_call(
-        functools.partial(scatter_kernel, sizes, orders),
-        in_specs=[pl.BlockSpec(memory_space=pl.ANY)] * number,
-        out_specs=[pl.BlockSpec(memory_space=pltpu.VMEM)] * number,
-        out_shape=[jax.ShapeDtypeStruct(shape, F32) for shape, _ in blocks],
+        functools.partial(products_kernel, sizes, tuple(jobs), tuple(messages), len(names), len(outs), len(rings)),
+        in_specs=[pl.BlockSpec(memory_space=pl.ANY)] * (len(names) + 1),
+        out_specs=[pl.BlockSpec(memory_space=pltpu.VMEM)] * len(outs),
+        out_shape=[jax.ShapeDtypeStruct(shape, F32) for shape in outs],
         scratch_shapes=[
             *scratch(0, False),
             *scratch(0, False),
             *scratch(1, True),
             *scratch(2, True),
             *scratch(3, True),
-            pltpu.SemaphoreType.DMA((number,)),
-            pltpu.SemaphoreType.DMA((number, slots)),
-            pltpu.SemaphoreType.DMA((number, slots)),
+            *[pltpu.VMEM((number, *sizes[:3], *shape), BF16) for number, *shape in rings],
+            pltpu.VMEM((2, deep, width), BF16),
+            pltpu.VMEM((2, deep, patch_width), BF16),
+            pltpu.VMEM((width, patch_width), F32),
+            pltpu.SemaphoreType.DMA((len(jobs), 2)),
+            pltpu.SemaphoreType.DMA,
+            pltpu.SemaphoreType.DMA((count, slots)),
+            pltpu.SemaphoreType.DMA((count, slots)),
         ],
         compiler_params=pltpu.CompilerParams(collective_id=1, has_side_effects=True, vmem_limit_bytes=VMEM_BYTES),
-        name="scatter_all",
-    )(*split)
+        name="weight_grads",
+    )(*inputs.values(), norm.reshape(*sizes, TILE_ROWS, LANES))
 
 
 GATHER_ORDERS = {
@@ -840,7 +977,7 @@
 
 
 def aligned(devices, shards):
-    return devices > 2 and devices % 2 == 0 and all(shard.shape[0] % TILE_ROWS == 0 for shard in shards.values())
+    return devices % 32 == 0 and all(shard.shape[0] % TILE_ROWS == 0 for shard in shards.values())
 
 
 def gather(devices, shards, norm):
@@ -857,33 +994,31 @@
     return {name: array[0] for name, array in zip(GATHER_ORDERS, fulls)}, norms
 
 
-SCATTER_ORDERS = {
-    "down": 0,
-    "up": 1,
-    "cross_key": 0,
-    "cross_value": 1,
-    "query": 0,
-    "key": 1,
-    "value": 0,
-    "out": 1,
-    "cross_query": 0,
-    "cross_out": 1,
-}
-
-
-def scatter(devices, shards, grads, norm):
+def scatter(devices, shards, inputs, norm):
+    width = inputs["tokens"].shape[1]
     if not aligned(devices, shards):
-        parts = [lax.psum_scatter(grads[name], "dp", scatter_dimension=0, tiled=True) for name in NAMES]
-        return [part.astype(F32) for part in parts], lax.psum_scatter(norm, "dp", scatter_dimension=1, tiled=True)
-    rows, width = norm.shape
-    width //= devices
-    norm = jnp.swapaxes(norm.reshape(rows, devices, width), 0, 1)
-    padded = jnp.zeros((devices, TILE_ROWS, LANES), F32).at[:, :rows, :width].set(norm)
-    blocks = [grads[name] for name in SCATTER_ORDERS] + [padded.reshape(devices * TILE_ROWS, LANES)]
-    orders = [ORDERS[at] for at in SCATTER_ORDERS.values()] + [ORDERS[0]]
-    *parts, norm = scatter_all(blocks, orders, devices)
-    parts = dict(zip(SCATTER_ORDERS, parts))
-    return [parts[name] for name in NAMES], norm[:rows, :width]
+        products = (
+            (inputs["grad_qkv"][:, :width], inputs["tokens"]),
+            (inputs["grad_qkv"][:, width : 2 * width], inputs["tokens"]),
+            (inputs["grad_qkv"][:, 2 * width :], inputs["tokens"]),
+            (inputs["branch_one"], inputs["mixed_self"]),
+            (inputs["grad_cross"], inputs["first_low"]),
+            (inputs["grad_keys"], inputs["padded"]),
+            (inputs["grad_values"], inputs["padded"]),
+            (inputs["branch_two"], inputs["mixed_cross"]),
+            (inputs["grad_pre"], inputs["second_low"]),
+            (inputs["branch_three"], inputs["hidden"]),
+        )
+        sums = [tn(left, right).astype(BF16) for left, right in products]
+        parts = [lax.psum_scatter(grad, "dp", scatter_dimension=0, tiled=True).astype(F32) for grad in sums]
+        return parts, lax.psum_scatter(norm, "dp", scatter_dimension=1, tiled=True)
+    rows = norm.shape[0]
+    columns = norm.shape[1] // devices
+    norm = jnp.swapaxes(norm.reshape(rows, devices, columns), 0, 1)
+    padded = jnp.zeros((devices, TILE_ROWS, LANES), F32).at[:, :rows, :columns].set(norm)
+    token, patch, up, down, norm = weight_grads(devices, inputs, padded)
+    parts = [token[0], token[1], token[2], token[3], token[4], patch[0], patch[1], token[5], up, down]
+    return parts, norm[:rows, :columns]
 
 
 def local(devices, text, patches, segment_ids, row_image, *rest):
@@ -938,20 +1073,24 @@
     )
     tokens = text.reshape(rows * length, width)
     patch_rows = padded.reshape(-1, padded.shape[-1])
-    products = (
-        (grad_qkv[:, :width], tokens),
-        (grad_qkv[:, width : 2 * width], tokens),
-        (grad_qkv[:, 2 * width :], tokens),
-        (branch_one, mixed_self),
-        (grad_cross, first_low),
-        (grad_keys.reshape(-1, width), patch_rows),
-        (grad_values.reshape(-1, width), patch_rows),
-        (branch_two, mixed_cross),
-        (grad_pre, second_low),
-        (branch_three, hidden),
-    )
-    sums = {name: tn(left, right).astype(BF16) for name, (left, right) in zip(NAMES, products, strict=True)}
-    grads, norm_grad = scatter(devices, shards, sums, (norm_late + norm_early)[:6])
+    inputs = {
+        "branch_three": branch_three,
+        "hidden": hidden,
+        "grad_pre": grad_pre,
+        "second_low": second_low,
+        "grad_keys": grad_keys.reshape(-1, width),
+        "grad_values": grad_values.reshape(-1, width),
+        "padded": patch_rows,
+        "branch_two": branch_two,
+        "mixed_cross": mixed_cross,
+        "grad_cross": grad_cross,
+        "first_low": first_low,
+        "branch_one": branch_one,
+        "mixed_self": mixed_self,
+        "grad_qkv": grad_qkv,
+        "tokens": tokens,
+    }
+    grads, norm_grad = scatter(devices, shards, inputs, (norm_late + norm_early)[:6])
     return (
         output.reshape(text.shape),
         text_grad.reshape(text.shape),

time: 523 us -> 441 us (0.84)
  matrix products: 44 us -> 0 us
  Pallas kernels: 451 us -> 423 us
  local copies, waits for them, and re-layouts: 20 us -> 10.2 us
    dot_general x10 -> x0, matrix products: 44 us -> none  [tn(): lax.dot_general(left, right, (((0,), (0,)), ((), ())), preferred_element_...]
    pallas_call x1, Pallas kernels: 141 us -> 114 us  [weight_grads(): pl.pallas_call(functools.partial(products_kernel, sizes, tuple(jobs), tup...]
    unnamed x45 -> x13, local copies, waits for them, and re-layouts: 16.2 us -> 2.95 us
where the time goes in v3:
time: 441 us; the launch traced here: 436 us
  Pallas kernels  423 us (96%)
  local copies, waits for them, and re-layouts  10.2 us (2%)
    pallas_call x1, Pallas kernels, weight_grads(): pl.pallas_call(functools.partial(products_kernel, sizes, tuple(jobs), tup...  114 us
    pallas_call x1, Pallas kernels, forward(): pl.pallas_call(functools.partial(forward_kernel, patch_count), grid_spec=...  104 us
    pallas_call x1, Pallas kernels, gather_all(): pl.pallas_call(functools.partial(gather_kernel, grid_of(devices), orders)...  97.4 us
    pallas_call x1, Pallas kernels, backward(): pl.pallas_call(backward_kernel, grid_spec=pltpu.PrefetchScalarGridSpec(nu...  86.5 us
    pallas_call x1, Pallas kernels, patch_grads(): pl.pallas_call(patch_kernel, grid=(images // IMAGE_BLOCK,), in_specs=[blo...  10.8 us
    pallas_call x1, Pallas kernels, image_rows(): pl.pallas_call(images_kernel, grid=(images // IMAGE_BLOCK,), in_specs=[bl...  10.1 us

profile of v3, /device:TPU:0, one launch (start us, length us, event | category | flops | bytes accessed | tf_op | source)
XLA Modules:
  0.0 436.2 jit_solution(15050638012069834073)
XLA Ops:
  0.7 1.3 scatter.6.refs_0_
  1.9 0.8 broadcast_add_fusion
  2.7 0.7 reshape.148.id_row_ref
  3.4 1.0 reshape.159.id_column_ref
  4.3 97.4 %gather_all.1 = (bf16[1,256,128]{2,1,0:T(8,128)(2,1)}, bf16[1,768,768]{2,1,0:T(8,128)(2,1)}, bf16[1,768,768]{2,1,0:T(8,128)(2,1)}, bf16[1,768,768]{2,1,0:T(8,128...) custom-call(bf16[1,8,128]{2,1,0:T(8,128)(2,1)} %scatter.6.refs_0_, ...), custom_call_target="tpu_custom_call" | custom-call | tf_op jit(solution)/shard_map/gather_all/pallas_call | solution.py:669
  101.7 0.8 copy.38
  102.6 0.1 convert_element_type.8
  102.7 0.6 pad_convert_fusion.norm_ref
  103.3 10.1 %image_rows.1 = (bf16[12,160,1024]{2,1,0:T(8,128)(2,1)}, bf16[12,160,768]{2,1,0:T(8,128)(2,1)}, bf16[12,160,768]{2,1,0:T(8,128)(2,1)}) custom-call(bf16[12,145,1024]{2,1,0:T(8,128)(2,1)} %patches_ref.1, bf16[768,1024]{1,0:T(8,128)(2,1)} %bitcast.92, bf16[768,1024]{1,0:T(8,128)(2,1)} %bitcast.94), custom_call_target="tpu_custom_call" | custom-call | tf_op jit(solution)/shard_map/image_rows/pallas_call | solution.py:99
  113.4 104.0 %forward.1 = (f32[960,768]{1,0:T(8,128)}, bf16[960,2304]{1,0:T(8,128)(2,1)}, bf16[12,6,160,80]{3,2,1,0:T(8,128)(2,1)}, bf16[960,768]{1,0:T(8,128)(2,1)}, f32[960...) custom-call(s32[24]{0:T(128)} %image_ref.3, ...), custom_call_target="tpu_custom_call" | custom-call | tf_op jit(solution)/shard_map/forward/pallas_call | solution.py:316
  217.4 0.0 copy-start.2
  217.4 86.5 %backward.1 = (f32[960,768]{1,0:T(8,128)}, bf16[960,768]{1,0:T(8,128)(2,1)}, bf16[960,768]{1,0:T(8,128)(2,1)}, bf16[960,768]{1,0:T(8,128)(2,1)}, bf16[960,2304]{...) custom-call(s32[24]{0:T(128)} %image_ref.3, ...), custom_call_target="tpu_custom_call" | custom-call | tf_op jit(solution)/shard_map/backward/pallas_call | solution.py:483
  303.9 0.0 copy-done.2
  303.9 0.7 slice_add_fusion
  304.7 0.1 reshape.157
  304.8 0.1 copy.36
  304.8 0.7 scatter.9.clone
  305.5 114.2 %weight_grads.1 = (f32[6,24,768]{2,1,0:T(8,128)}, f32[2,24,1024]{2,1,0:T(8,128)}, f32[96,768]{1,0:T(8,128)}, f32[24,3072]{1,0:T(8,128)}, f32[8,128]{1,0:T(8,128)}) custom-call(bf16[960,768]{1,0:T(8,128)(2,1)} %get-tuple-element.105.refs_0_, bf16[960,3072]{1,0:T(8,128)(2,1)} %get-tuple-element.106.refs_1_, bf16[960,3072]{1,0:T(8,128)(2,1)} %get-tuple-element.107.refs_2_, ...), custom_call_target="tpu_custom_call" | custom-call | tf_op jit(solution)/shard_map/weight_grads/pallas_call | solution.py:940
  419.8 1.8 slice_bitcast_fusion.2
  421.6 1.6 slice_bitcast_fusion
  423.2 0.0 copy-start.1
  423.2 0.0 copy-start
  423.2 0.0 copy-start.3
  423.2 10.8 %patch_grads.1 = f32[12,145,1024]{2,1,0:T(8,128)} custom-call(bf16[12,160,768]{2,1,0:T(8,128)(2,1)} %get-tuple-element.103.keys_ref, bf16[12,160,768]{2,1,0:T(8,128)(2,1)} %get-tuple-element.104.values_ref, bf16[768,1024]{1,0:T(8,128)(2,1)} %bitcast.93, bf16[768,1024]{1,0:T(8,128)(2,1)} %bitcast.95), custom_call_target="tpu_custom_call" | custom-call | tf_op jit(solution)/shard_map/patch_grads/pallas_call | solution.py:127
  434.0 0.0 copy-done.1
  434.0 0.7 copy.42
  434.7 0.0 copy-done
  434.7 0.7 copy.43
  435.5 0.0 copy-done.3
  435.5 0.6 copy.44
  (1 shorter events, 0.0 us)
Async XLA Ops:
  217.4 86.5 %copy-start.2 = (f32[8,768]{1,0:T(8,128)S(1)}, f32[8,768]{1,0:T(8,128)}, u32[]{:S(2)}) copy-start(f32[8,768]{1,0:T(8,128)} %get-tuple-element.117) | copy-start | bytes 73732
  423.2 10.8 %copy-start.1 = (f32[96,768]{1,0:T(8,128)S(1)}, f32[96,768]{1,0:T(8,128)}, u32[]{:S(2)}) copy-start(f32[96,768]{1,0:T(8,128)} %get-tuple-element.121) | copy-start | bytes 884740
  423.2 11.5 %copy-start = (f32[24,3072]{1,0:T(8,128)S(1)}, f32[24,3072]{1,0:T(8,128)}, u32[]{:S(2)}) copy-start(f32[24,3072]{1,0:T(8,128)} %get-tuple-element.122) | copy-start | bytes 884740
  423.2 12.2 %copy-start.3 = (f32[8,128]{1,0:T(8,128)S(1)}, f32[8,128]{1,0:T(8,128)}, u32[]{:S(2)}) copy-start(f32[8,128]{1,0:T(8,128)} %get-tuple-element.123) | copy-start | bytes 12292
